TPU v7x, 256 devices: a whole 4x4x8 slice. The times are simulated.
256 devices in a mesh: facet: 128 (over x, z, y), half: 2 (over core).
Axes of the slice: x: 4, y: 4, z: 8, core: 2. Of those that a mesh axis runs over, the one named last changes fastest.
Arguments:
- facet_image: bfloat16 [128, 2048, 2048], P('facet', 'half'), may hold values from -6 to 6
- coverage: int32 [128, 8], P('facet'), may hold values 0 or 1
- row_offsets: int32 [8], replicated, may hold values from 0 to 131071
- column_offset: int32 [1], replicated, may hold values from 0 to 131071
- piece_owner: int32 [2, 128], replicated, may hold values from 0 to 127, as said below
Outputs:
- subgrid_slots: float32 [2, 128, 3, 2, 16, 512], P('half', 'facet')
Inputs may be any that keep to these rules, and one draw needn't show every extreme that they name: `piece_owner`: for each half, every owner index names at most 3 of the 128 pieces, and some owner names exactly 3.
All inputs are finite; a program needn't handle non-finite values. No bound on the sum of `coverage` on one device may be relied on, other than what follows from the above.
Results may differ from a plain program's by a relative error of at most 0.0077.
Values may be sent and summed in bfloat16 or wider, within the bound.
No kernel may reach another device: no remote copies, remote signals or barrier semaphores. Data moves between devices by JAX's collectives and lax.ppermute only.
A program may use at most 64 MiB of HBM per device.

v0:
```python
import math

import jax
import jax.numpy as jnp
from jax import lax
from jax.sharding import PartitionSpec as P

FS = 2048
M = 256
SG = 512
IMAGE = 131072
SUBGRIDS = 8
CAP = 3


TWO_PI = 2.0 * math.pi


def window_table(positions, offset, samples):
    stride = IMAGE // FS
    ticks = (jnp.arange(samples, dtype=jnp.int32) - samples // 2) * stride
    shifted = jnp.mod(offset + ticks, IMAGE)
    product = jnp.mod(positions[:, None] * shifted[None, :], IMAGE)
    phases = -TWO_PI / IMAGE * product.astype(jnp.float32)
    relative = positions.astype(jnp.float32) * (2.0 / FS)
    taper = jnp.exp(-2.0 * relative * relative) / math.sqrt(FS)
    return (taper[:, None] * jnp.cos(phases), taper[:, None] * jnp.sin(phases))


def facet_shift(facet_id):
    ratio = IMAGE // FS
    shift_a = jnp.mod(7 * facet_id, ratio) - ratio // 2
    shift_b = jnp.mod(5 * (facet_id // ratio) + 3 * facet_id, ratio) - ratio // 2
    return (shift_a, shift_b)


def long_phase(shift, offset, samples):
    stride = IMAGE // FS
    ticks = (jnp.arange(samples, dtype=jnp.int32) - samples // 2) * stride
    wrapped = jnp.mod(offset + ticks, IMAGE)
    scaled = jnp.mod(FS * wrapped, IMAGE)
    product = jnp.mod(shift * scaled, IMAGE)
    phases = -TWO_PI / IMAGE * product.astype(jnp.float32)
    return (jnp.cos(phases), jnp.sin(phases))


def grid_table():
    ticks_in = jnp.arange(M, dtype=jnp.int32) - M // 2
    ticks_out = jnp.arange(SG, dtype=jnp.int32) - SG // 2
    product = jnp.mod(ticks_in[:, None] * ticks_out[None, :], SG)
    phases = TWO_PI / SG * product.astype(jnp.float32)
    return (jnp.cos(phases) / math.sqrt(M), jnp.sin(phases) / math.sqrt(M))


def weighted_parts(part_re, part_im, cover, offsets, column, facet_id):
    shift_a, shift_b = facet_shift(facet_id)
    rot_re, rot_im = long_phase(shift_a, offsets[:, None], M)
    scaled_re = cover[:, None, None] * (rot_re[:, :, None] * part_re - rot_im[:, :, None] * part_im)
    scaled_im = cover[:, None, None] * (rot_re[:, :, None] * part_im + rot_im[:, :, None] * part_re)
    col_re, col_im = long_phase(shift_b, column, M)
    grid_re, grid_im = grid_table()
    tilt_re = col_re[:, None] * grid_re - col_im[:, None] * grid_im
    tilt_im = col_re[:, None] * grid_im + col_im[:, None] * grid_re
    return (
        scaled_re.astype(jnp.bfloat16),
        scaled_im.astype(jnp.bfloat16),
        tilt_re.astype(jnp.bfloat16),
        tilt_im.astype(jnp.bfloat16),
    )


def to_subgrid(summed, out_table):
    item_count = summed.shape[0]
    width_cols = summed.shape[2]
    real_part = jnp.dot(
        summed[:, 0].reshape(item_count * width_cols, M),
        out_table,
        preferred_element_type=jnp.float32,
    )
    imag_part = jnp.dot(
        summed[:, 1].reshape(item_count * width_cols, M),
        out_table,
        preferred_element_type=jnp.float32,
    )
    out_re = (real_part[:, :SG] - imag_part[:, SG:]).reshape(item_count, width_cols, SG)
    out_im = (real_part[:, SG:] + imag_part[:, :SG]).reshape(item_count, width_cols, SG)
    return jnp.stack([out_re, out_im], axis=1)


def slot_index(owners):
    positions = jnp.arange(owners.shape[0], dtype=jnp.int32)
    same_owner = owners[:, None] == owners[None, :]
    earlier = positions[:, None] > positions[None, :]
    return jnp.sum((same_owner & earlier).astype(jnp.int32), axis=1)


def slot_source(owners, slot_of, targets):
    positions = jnp.arange(owners.shape[0], dtype=jnp.int32)
    levels = jnp.arange(CAP, dtype=jnp.int32)
    matches = (owners[None, None, :] == targets[:, None, None]) & (
        slot_of[None, None, :] == levels[None, :, None]
    )
    source = jnp.sum(jnp.where(matches, positions[None, None, :], 0), axis=2)
    filled = jnp.any(matches, axis=2)
    return (source, filled)


def split_parts(blocks):
    part_re = blocks[:, :M, :M] - blocks[:, M:, M:]
    part_im = blocks[:, :M, M:] + blocks[:, M:, :M]
    return jnp.stack([part_re, part_im], axis=1)


def shards(facet_image, coverage, row_offsets, column_offset, piece_owner):
    halves = lax.axis_size("half")
    facets = lax.axis_size("facet")
    half_id = lax.axis_index("half")
    facet_id = lax.axis_index("facet")
    pixels = facet_image[0]
    local_rows = pixels.shape[0]
    row_place = half_id * local_rows + jnp.arange(local_rows, dtype=jnp.int32) - FS // 2
    col_place = jnp.arange(FS, dtype=jnp.int32) - FS // 2
    col_re, col_im = window_table(col_place, column_offset[0], M)
    col_table = jnp.concatenate([col_re, col_im], axis=1).astype(jnp.bfloat16)
    folded = jnp.dot(pixels, col_table, preferred_element_type=jnp.float32).astype(jnp.bfloat16)
    per_half = SUBGRIDS // halves
    offsets_mine = lax.dynamic_slice_in_dim(row_offsets, half_id * per_half, per_half, 0)

    def row_one(offset_one):
        table_re, table_im = window_table(row_place, offset_one, M)
        return jnp.concatenate([table_re, table_im], axis=1)

    row_table = jax.vmap(row_one)(row_offsets).astype(jnp.bfloat16)
    blocks = jnp.einsum("sra,rb->sab", row_table, folded, preferred_element_type=jnp.float32)
    stacked = split_parts(blocks)
    whole_sum = lax.psum(stacked, "half")
    local_part = lax.dynamic_slice_in_dim(whole_sum, half_id * per_half, per_half, 0)
    cover_mine = lax.dynamic_slice_in_dim(coverage[0], half_id * per_half, per_half, 0).astype(
        jnp.float32
    )
    y_re, y_im, tilt_re, tilt_im = weighted_parts(
        local_part[:, 0], local_part[:, 1], cover_mine, offsets_mine, column_offset[0], facet_id
    )
    width_cols = SG * per_half // facets
    blocks_per = SG // width_cols
    tilt_re = tilt_re.reshape(M, blocks_per, width_cols)
    tilt_im = tilt_im.reshape(M, blocks_per, width_cols)
    piece_re = jnp.einsum(
        "lbj,skl->sbjk", tilt_re, y_re, preferred_element_type=jnp.float32
    ) - jnp.einsum("lbj,skl->sbjk", tilt_im, y_im, preferred_element_type=jnp.float32)
    piece_im = jnp.einsum(
        "lbj,skl->sbjk", tilt_re, y_im, preferred_element_type=jnp.float32
    ) + jnp.einsum("lbj,skl->sbjk", tilt_im, y_re, preferred_element_type=jnp.float32)
    pieces = (
        jnp.stack([piece_re, piece_im], axis=2)
        .astype(jnp.bfloat16)
        .reshape(facets, 2, width_cols, M)
    )
    owners = lax.dynamic_index_in_dim(piece_owner, half_id, 0, keepdims=False)
    slot_of = slot_index(owners)
    grid_re, grid_im = grid_table()
    out_table = jnp.concatenate([grid_re, grid_im], axis=1).astype(jnp.bfloat16)
    factor = 1.0 / math.sqrt(facets)
    targets = jnp.arange(facets, dtype=jnp.int32)
    source, filled = slot_source(owners, slot_of, targets)
    outbox = jnp.where(filled[:, :, None, None, None], pieces[source], jnp.zeros((), jnp.bfloat16))
    result = to_subgrid(
        (
            jnp.sum(
                lax.all_to_all(outbox, "facet", split_axis=0, concat_axis=0, tiled=True),
                axis=0,
                dtype=jnp.float32,
            )
            * factor
        ).astype(jnp.bfloat16),
        out_table,
    )
    return result[None, None]


def solution(mesh):
    return jax.shard_map(
        shards,
        mesh=mesh,
        in_specs=(P("facet", "half", None), P("facet", None), P(), P(), P()),
        out_specs=P("half", "facet", None, None, None, None),
        check_vma=False,
    )
```

profile of v0, /device:TPU:8, one launch (start us, length us, event | category | flops | bytes accessed | tf_op | source)
XLA Modules:
  0.0 310.7 jit_solution(17229152549467784683)
XLA Ops:
  7.3 0.7 add_select_fusion.5
  8.0 10.0 %multiply_convert_fusion.3 = (bf16[2048,256]{1,0:T(8,128)(2,1)S(1)}, bf16[2048,256]{1,0:T(8,128)(2,1)S(1)}) fusion(s32[256]{0:T(256)S(1)} %and_select_fusion.3, s32[2048]{0:T(1024)S(1)} %iota_add_fusion, f32[2048]{0:T(1024)S(1)} %exponential_multiply_fusion), kind=kLoop, calls=%fused_computation.39 | loop fusion | flops 9437184 | bytes 2114560 | tf_op jit(solution)/shard_map/convert.8
  18.0 4.6 %fusion.22 = bf16[512,1024,1]{1,0,2:T(8,128)(2,1)S(1)} fusion(bf16[1,1024,2048]{2,1,0:T(8,128)(2,1)} %param.5, bf16[2048,256]{1,0:T(8,128)(2,1)S(1)} %get-tuple-element.14, bf16[2048,256]{1,0:T(8,128)(2,1)S(1)} %get-tuple-element.13), kind=kOutput, calls=%fused_computation.41 | convolution fusion | flops 2152202240 | bytes 7340032 | tf_op jit(solution)/shard_map/dot_general | solution.py:125
  22.6 35.4 %multiply_convert_fusion.1 = (bf16[8,1024,256]{1,2,0:T(8,128)(2,1)S(1)}, bf16[8,1024,256]{1,2,0:T(8,128)(2,1)S(1)}) fusion(s32[8,256]{1,0:T(8,128)S(1)} %add_select_fusion.5, s32[1024]{0:T(1024)S(1)} %add_add_fusion.1, f32[1024]{0:T(1024)S(1)} %exponential_multiply_fusion.1), kind=kLoop, calls=%fused_computation.15 | loop fusion | flops 37748736 | bytes 8404992 | tf_op jit(solution)/shard_map/convert.10
  58.1 4.6 %fusion.3 = f32[8,512,512]{2,1,0:T(8,128)S(1)} fusion(bf16[512,1024,1]{1,0,2:T(8,128)(2,1)S(1)} %fusion.22, bf16[8,1024,256]{1,2,0:T(8,128)(2,1)S(1)} %get-tuple-element.16, bf16[8,1024,256]{1,2,0:T(8,128)(2,1)S(1)} %get-tuple-element.15), kind=kOutput, calls=%fused_computation.10 | convolution fusion | flops 4311744512 | bytes 17825792 | tf_op jit(solution)/shard_map/sra,rb->sab/dot_general | solution.py:134
  62.6 0.5 fusion.13
  63.2 2.4 pad_maximum_fusion
  65.6 0.6 copy-done.1
  66.8 0.2 reshape.377
  67.6 39.9 %all-reduce.2.cloned.1.call-done = f32[8,2,256,256]{3,2,0,1:T(8,128)} async-done(((f32[8,2,256,256]{3,2,0,1:T(8,128)}), f32[8,2,256,256]{3,2,0,1:T(8,128)}) %all-reduce.2.cloned.1.call-update) | async-done | bytes 4194320 | tf_op jit(solution)/shard_map/psum | solution.py:136
  107.5 1.9 fusion.35
  109.5 2.5 fusion.45
  111.9 2.5 fusion.47
  114.4 3.4 %fusion.28 = bf16[4,32,16,256]{3,1,2,0:T(8,128)(2,1)S(1)} fusion(f32[4,256,32,16]{1,2,3,0:T(8,128)S(1)} %fusion.45, bf16[4,256,256,1]{2,1,3,0:T(8,128)(2,1)S(1)} %get-tuple-element.7, f32[256]{0:T(256)S(1)} %get-tuple-element.21, f32[256]{0:T(256)S(1)} %get-tuple-element.22, s32[32,16]{0,1:T(8,128)S(1)} %add_add_fusion, s32[256]{0:T(256)S(1)} %iota_add_fusion.2), kind=kOutput, calls=%fused_computation.43 | convolution fusion | flops 271843328 | bytes 3675136 | tf_op jit(solution)/shard_map/lbj,skl->sbjk/dot_general | solution.py:153
  117.7 0.6 copy.14
  118.3 3.1 %fusion.27 = bf16[4,32,16,256]{3,1,2,0:T(8,128)(2,1)S(1)} fusion(f32[4,256,32,16]{1,2,3,0:T(8,128)S(1)} %fusion.47, bf16[4,256,256,1]{2,1,3,0:T(8,128)(2,1)S(1)} %get-tuple-element.8, f32[256]{0:T(256)S(1)} %get-tuple-element.21, f32[256]{0:T(256)S(1)} %get-tuple-element.22, s32[32,16]{0,1:T(8,128)S(1)} %add_add_fusion, s32[256]{0:T(256)S(1)} %iota_add_fusion.2), kind=kOutput, calls=%fused_computation.42 | convolution fusion | flops 271843328 | bytes 3675136 | tf_op jit(solution)/shard_map/lbj,skl->sbjk/dot_general | solution.py:150
  121.5 0.6 copy.13
  122.3 13.2 %gather_fusion = bf16[384,2,16,256]{3,2,1,0:T(8,128)(2,1)} fusion(bf16[128,2,16,256]{3,2,0,1:T(8,128)(2,1)S(1)} %pad_maximum_fusion.1, s32[1024]{0:T(1024)S(1)} %pad_clamp_fusion), kind=kCustom, calls=%fused_computation | custom fusion | bytes 12584448 | tf_op jit(solution)/shard_map/gather | solution.py:166
  135.5 6.7 %broadcast_select_fusion = bf16[128,3,2,16,256]{4,3,2,1,0:T(8,128)(2,1)} fusion(bf16[128,3,2,16,256]{4,3,2,1,0:T(8,128)(2,1)} %bitcast.66, pred[128,3]{1,0:T(8,128)(4,1)S(1)} %copy.12), kind=kLoop, calls=%fused_computation.16 | loop fusion | flops 3145728 | bytes 12583296 | tf_op jit(solution)/shard_map/jit(_where)/select_n | solution.py:166
  142.2 14.2 %all-to-all-start = ((bf16[128,3,2,16,256]{4,3,2,1,0:T(8,128)(2,1)}), bf16[128,3,2,16,256]{4,3,2,1,0:T(8,128)(2,1)}, u32[]{:S(2)}, u32[]{:S(2)}) async-start(bf16[128,3,2,16,256]{4,3,2,1,0:T(8,128)(2,1)} %broadcast_select_fusion), calls=%async_computation | async-start | bytes 12582912 | tf_op jit(solution)/shard_map/all_to_all | solution.py:170
  156.3 2.5 multiply_convert_fusion.7
  158.8 139.9 %all-to-all-done = bf16[128,3,2,16,256]{4,3,2,1,0:T(8,128)(2,1)} async-done(((bf16[128,3,2,16,256]{4,3,2,1,0:T(8,128)(2,1)}), bf16[128,3,2,16,256]{4,3,2,1,0:T(8,128)(2,1)}, u32[]{:S(2)}, u32[]{:S(2)}) %all-to-all-start) | async-done | bytes 6291488 | tf_op jit(solution)/shard_map/all_to_all | solution.py:170
  298.7 4.0 %convert_reduce_fusion = f32[3,2,16,256]{3,2,1,0:T(8,128)S(1)} fusion(bf16[128,3,2,16,256]{4,3,2,1,0:T(8,128)(2,1)} %all-to-all-done), kind=kLoop, calls=%fused_computation.4 | loop fusion | flops 6266880 | bytes 6389760 | tf_op jit(solution)/shard_map/reduce_sum | solution.py:169
  303.2 0.7 maximum_bitcast_fusion
  (36 shorter events, 1.9 us)
Async XLA Ops:
  6.5 59.8 %copy-start = (s32[2,128]{1,0:T(2,128)S(1)}, s32[2,128]{1,0:T(2,128)}, u32[]{:S(2)}) copy-start(s32[2,128]{1,0:T(2,128)} %param.9) | copy-start | bytes 3076
  6.5 101.0 %all-reduce.2.cloned.1.call-start = ((), (), s32[]{:S(2)}) async-start(), calls=%async_computation.1 | async-start | bytes 8388608 | tf_op jit(solution)/shard_map/psum | solution.py:136
  65.6 0.7 copy-start.1
  65.6 1.7 copy-start.2
  142.2 156.6 %all-to-all-start = ((bf16[128,3,2,16,256]{4,3,2,1,0:T(8,128)(2,1)}), bf16[128,3,2,16,256]{4,3,2,1,0:T(8,128)(2,1)}, u32[]{:S(2)}, u32[]{:S(2)}) async-start(bf16[128,3,2,16,256]{4,3,2,1,0:T(8,128)(2,1)} %broadcast_select_fusion), calls=%async_computation | async-start | bytes 12582912 | tf_op jit(solution)/shard_map/all_to_all | solution.py:170
Sparse Core Ops, SparseCore 0:
  65.7 41.7 all-reduce.1
where the time goes:
time: 311 us
  waiting for transfers between devices  180 us (58%)
  other arithmetic  66 us (21%)
  matrix products  20.9 us (7%)
  local copies, waits for them, and re-layouts  15.5 us (5%)
  between operations  14.3 us (5%)
  starting transfers between devices  14.2 us (5%)
    all_to_all x1, waiting for transfers between devices, shards(): lax.all_to_all(outbox, 'facet', split_axis=0, concat_axis=0, tiled=True)  140 us
    another operation x3, other arithmetic  47.9 us
    psum x1, waiting for transfers between devices, shards(): whole_sum = lax.psum(stacked, 'half')  39.9 us
    all_to_all x1, starting transfers between devices, shards(): lax.all_to_all(outbox, 'facet', split_axis=0, concat_axis=0, tiled=True)  14.2 us
    gather x1, local copies, waits for them, and re-layouts, shards(): pieces[source]  13.2 us
    select_n x1, other arithmetic, shards(): jnp.where(filled[:, :, None, None, None], pieces[source], jnp.zeros((), j...  6.68 us
  transfers between devices with their start and end apart: 2, of which 2 were waited for; matrix products, arithmetic and copies ran while one was open for 1% of the time, Pallas kernels for 0%

commit v1 on v0

v1 whole, which is shorter than its diff:
```python
import math

import jax
import jax.numpy as jnp
from jax import lax
from jax.sharding import PartitionSpec as P

FS = 2048
M = 256
SG = 512
IMAGE = 131072
SUBGRIDS = 8
CAP = 3
NX, NZ, NY = 4, 8, 4
GROUP = NX * NY
KB = M // GROUP
FINE = 16

TWO_PI = 2.0 * math.pi
STRIDE = IMAGE // FS


def unit(product, period, sign=-1.0):
    phases = (sign * TWO_PI / period) * jnp.mod(product, period).astype(jnp.float32)
    return jnp.cos(phases), jnp.sin(phases)


def cmul(a, b):
    return a[0] * b[0] - a[1] * b[1], a[0] * b[1] + a[1] * b[0]


def taper_of(place):
    relative = place.astype(jnp.float32) * (2.0 / FS)
    return jnp.exp(-2.0 * relative * relative) / math.sqrt(FS)


def fourier(coarse, samples=M):
    ticks = jnp.arange(samples, dtype=jnp.int32) - samples // 2
    big = unit(coarse[:, None] * ticks[None, :], FS)
    fine = jnp.arange(FINE, dtype=jnp.int32)
    small = unit(fine[:, None] * ticks[None, :], FS)
    return cmul(
        (big[0][:, None, :], big[1][:, None, :]), (small[0][None], small[1][None])
    )


def window(coarse, offsets):
    fine = jnp.arange(FINE, dtype=jnp.int32)
    place = coarse[:, None] + fine[None, :]
    taper = taper_of(place)
    turn = unit(place[None] * offsets[:, None, None], IMAGE)
    gain = (taper * turn[0])[..., None], (taper * turn[1])[..., None]
    base = fourier(coarse)
    table = cmul(gain, (base[0][None], base[1][None]))
    rows = coarse.shape[0] * FINE
    return [t.reshape(offsets.shape[0], rows, M).astype(jnp.bfloat16) for t in table]


def grid_table():
    ticks_in = jnp.arange(M, dtype=jnp.int32) - M // 2
    ticks_out = jnp.arange(SG, dtype=jnp.int32) - SG // 2
    grid = unit(ticks_in[:, None] * ticks_out[None, :], SG, 1.0)
    return [(g / math.sqrt(M)).astype(jnp.bfloat16) for g in grid]


def facet_weight(facet_id, offsets, column, cover):
    ratio = STRIDE
    shift_a = jnp.mod(7 * facet_id, ratio) - ratio // 2
    shift_b = jnp.mod(5 * (facet_id // ratio) + 3 * facet_id, ratio) - ratio // 2
    turn = shift_a * jnp.mod(FS * offsets, IMAGE) + shift_b * jnp.mod(FS * column, IMAGE)
    w = unit(turn, IMAGE)
    return cover * w[0], cover * w[1]


def dot(spec, a, b):
    return jnp.einsum(spec, a, b, preferred_element_type=jnp.float32)


def shards(facet_image, coverage, row_offsets, column_offset, piece_owner):
    half = lax.axis_index("half")
    facet_id = lax.axis_index("facet")
    pixels = facet_image[0]
    local_rows = FS // 2
    per_half = SUBGRIDS // 2
    offsets = lax.dynamic_slice_in_dim(row_offsets, half * per_half, per_half, 0)
    cover = lax.dynamic_slice_in_dim(coverage[0], half * per_half, per_half, 0)

    coarse = FINE * jnp.arange(FS // FINE, dtype=jnp.int32) - FS // 2
    col = window(coarse, column_offset)
    col = jnp.concatenate([col[0][0], col[1][0]], axis=1)
    folded = jnp.dot(pixels, col, preferred_element_type=jnp.float32).astype(jnp.bfloat16)
    other = lax.ppermute(folded, "half", [(0, 1), (1, 0)])

    def part_of(which, block):
        first = FINE * jnp.arange(local_rows // FINE, dtype=jnp.int32)
        row = window(first + which * local_rows - FS // 2, offsets)
        row = jnp.concatenate(row, axis=2)
        return dot("sra,rb->sab", row, block)

    blocks = part_of(half, folded) + part_of(1 - half, other)
    part = (
        blocks[:, :M, :M] - blocks[:, M:, M:],
        blocks[:, :M, M:] + blocks[:, M:, :M],
    )
    w = facet_weight(facet_id, offsets, column_offset[0], cover.astype(jnp.float32))
    y = cmul((w[0][:, None, None], w[1][:, None, None]), part)
    y = jnp.stack(y, axis=1).astype(jnp.bfloat16)
    y = y.reshape(per_half, 2, GROUP, KB, M).transpose(2, 0, 1, 3, 4)
    groups = [
        [(x * NZ + z) * NY + v for x in range(NX) for v in range(NY)] for z in range(NZ)
    ]
    y = lax.all_to_all(
        y, "facet", split_axis=0, concat_axis=0, axis_index_groups=groups, tiled=True
    )
    y = jnp.sum(y, axis=0, dtype=jnp.float32).astype(jnp.bfloat16)

    grid = grid_table()
    wide = jnp.concatenate(grid, axis=1)
    full = dot("sckl,lj->sckj", y, wide)
    spread = jnp.stack(
        [
            full[:, 0, :, :SG] - full[:, 1, :, SG:],
            full[:, 0, :, SG:] + full[:, 1, :, :SG],
        ],
        axis=1,
    ).astype(jnp.bfloat16)
    width = 16
    blocks_per = SG // width
    pieces = spread.reshape(per_half, 2, KB, blocks_per, width)
    pieces = pieces.transpose(0, 3, 1, 2, 4).reshape(per_half * blocks_per, 2 * KB * width)

    owners = lax.dynamic_index_in_dim(piece_owner, half, 0, keepdims=False)
    count = owners.shape[0]
    place = jnp.arange(count, dtype=jnp.int32)
    same = (owners[:, None] == owners[None, :]) & (place[:, None] < place[None, :])
    slot_of = jnp.sum(same.astype(jnp.int32), axis=0)
    target = jnp.arange(count * CAP, dtype=jnp.int32)
    pick = (target[:, None] == (owners * CAP + slot_of)[None, :]).astype(jnp.bfloat16)
    outbox = jnp.dot(pick, pieces, preferred_element_type=jnp.float32)
    outbox = outbox.astype(jnp.bfloat16).reshape(count, CAP * 2 * KB * width // 128, 128)
    inbox = lax.all_to_all(outbox, "facet", split_axis=0, concat_axis=0, tiled=True)

    inbox = inbox.reshape(NX, NZ, NY, CAP, 2, KB, width)
    summed = jnp.sum(inbox, axis=1, dtype=jnp.float32) * (1.0 / math.sqrt(count))
    summed = summed.astype(jnp.bfloat16).transpose(2, 3, 5, 0, 1, 4)
    summed = summed.reshape(CAP, 2, width, M)
    out = dot("cdjk,ki->cdji", summed, wide)
    out_re = out[:, 0, :, :SG] - out[:, 1, :, SG:]
    out_im = out[:, 0, :, SG:] + out[:, 1, :, :SG]
    return jnp.stack([out_re, out_im], axis=1)[None, None]


def solution(mesh):
    return jax.shard_map(
        shards,
        mesh=mesh,
        in_specs=(P("facet", "half", None), P("facet", None), P(), P(), P()),
        out_specs=P("half", "facet", None, None, None, None),
        check_vma=False,
    )
```

time: 311 us -> 96.1 us (0.31)
  waiting for transfers between devices: 180 us -> 14.5 us
  other arithmetic: 66 us -> 18.3 us
  blocking collectives: 0 us -> 30.7 us
  between operations: 14.3 us -> 0.98 us
  matrix products: 20.9 us -> 11.3 us
  starting transfers between devices: 14.2 us -> 7.4 us
    all_to_all x1, waiting for transfers between devices: 140 us -> 14.5 us  [shards(): lax.all_to_all(y, 'facet', split_axis=0, concat_axis=0, axis_index_groups...]
    another operation x6 -> x2, other arithmetic: 51 us -> 0.52 us
    psum x1 -> x0, waiting for transfers between devices: 39.9 us -> none  [shards(): whole_sum = lax.psum(stacked, 'half')]
    all_to_all x0 -> x1, blocking collectives: none -> 30.7 us  [shards(): lax.all_to_all(outbox, 'facet', split_axis=0, concat_axis=0, tiled=True)]
    gather x1 -> x0, local copies, waits for them, and re-layouts: 13.2 us -> none  [shards(): pieces[source]]
    dot_general x8 -> x6, matrix products: 20.9 us -> 11.3 us  [the longest x4 7.66 us: dot(): return jnp.einsum(spec, a, b, preferred_element_type=jnp.float32)]
    select_n x4 -> x0, other arithmetic: 7.44 us -> none  [the longest x1 6.68 us: shards(): jnp.where(filled[:, :, None, None, None], pieces[source], jnp.zeros((), j...]
    all_to_all x1, starting transfers between devices: 14.2 us -> 7.39 us  [shards(): lax.all_to_all(y, 'facet', split_axis=0, concat_axis=0, axis_index_groups...]
  transfers between devices with their start and end apart: 2 -> 2, of which waited for: 2 -> 1; matrix products, arithmetic and copies ran while one was open for 1% -> 18% of each run, Pallas kernels for 0% -> 0%
where the time goes in v1:
time: 96.1 us; the launch traced here: 95.7 us
  blocking collectives  30.7 us (32%)
  other arithmetic  18.3 us (19%)
  waiting for transfers between devices  14.5 us (15%)
  local copies, waits for them, and re-layouts  12.6 us (13%)
  matrix products  11.3 us (12%)
  starting transfers between devices  7.4 us (8%)
  between operations  0.98 us (1%)
    all_to_all x1, blocking collectives, shards(): lax.all_to_all(outbox, 'facet', split_axis=0, concat_axis=0, tiled=True)  30.7 us
    all_to_all x1, waiting for transfers between devices, shards(): lax.all_to_all(y, 'facet', split_axis=0, concat_axis=0, axis_index_groups...  14.5 us
    dot_general x4, matrix products, dot(): return jnp.einsum(spec, a, b, preferred_element_type=jnp.float32)  7.66 us
    all_to_all x1, starting transfers between devices, shards(): lax.all_to_all(y, 'facet', split_axis=0, concat_axis=0, axis_index_groups...  7.39 us
    convert_element_type x3, other arithmetic, window(): t.reshape(offsets.shape[0], rows, M).astype(jnp.bfloat16)  4.82 us
    reduce_sum x1, other arithmetic, shards(): jnp.sum(inbox, axis=1, dtype=jnp.float32) * (1.0 / math.sqrt(count))  3.67 us
    convert_element_type x1, local copies, waits for them, and re-layouts, shards(): jnp.sum(inbox, axis=1, dtype=jnp.float32) * (1.0 / math.sqrt(count))  3.59 us
    dot_general x1, matrix products, shards(): jnp.dot(pixels, col, preferred_element_type=jnp.float32)  3.37 us
  transfers between devices with their start and end apart: 2, of which 1 were waited for; matrix products, arithmetic and copies ran while one was open for 18% of the time, Pallas kernels for 0%

profile of v1, /device:TPU:8, one launch (start us, length us, event | category | flops | bytes accessed | tf_op | source)
XLA Modules:
  0.0 95.7 jit_solution(5524475314059644457)
XLA Ops:
  0.1 0.6 fusion.47
  1.8 0.6 multiply_subtract_fusion
  2.5 1.0 %fusion.14 = (bf16[2048,256]{1,0:T(8,128)(2,1)S(1)}, bf16[2048,256]{1,0:T(8,128)(2,1)S(1)}) fusion(f32[128,16,256]{2,1,0:T(8,128)S(1)} %get-tuple-element.21, f32[128,16,256]{2,1,0:T(8,128)S(1)} %get-tuple-element.20, f32[2048]{0:T(1024)S(1)} %get-tuple-element.29, f32[2048]{0:T(1024)S(1)} %get-tuple-element.28), kind=kLoop, calls=%fused_computation.20 | loop fusion | flops 4194304 | bytes 6307840 | tf_op jit(solution)/shard_map/convert_element_type | solution.py:56
  3.5 1.2 %copy-done.3 = bf16[1,1024,2048]{2,1,0:T(8,128)(2,1)S(1)} copy-done((bf16[1,1024,2048]{2,1,0:T(8,128)(2,1)S(1)}, bf16[1,1024,2048]{2,1,0:T(8,128)(2,1)}, u32[]{:S(2)}) %copy-start.3) | copy-done | bytes 4194328
  4.6 3.4 %fusion.20 = bf16[512,1024]{1,0:T(8,128)(2,1)} fusion(bf16[1,1024,2048]{2,1,0:T(8,128)(2,1)S(1)} %copy-done.3, bf16[2048,256]{1,0:T(8,128)(2,1)S(1)} %get-tuple-element.9, bf16[2048,256]{1,0:T(8,128)(2,1)S(1)} %get-tuple-element.8), kind=kOutput, calls=%fused_computation.28 | convolution fusion | flops 2152202240 | bytes 7340032 | tf_op jit(solution)/shard_map/dot_general | solution.py:91
  8.2 0.6 fusion.50
  9.0 1.6 %multiply_subtract_fusion.1 = (f32[64,16,256]{2,1,0:T(8,128)S(1)}, f32[64,16,256]{2,1,0:T(8,128)S(1)}, f32[64,16,256]{2,1,0:T(8,128)S(1)}, f32[64,16,256]{2,1,0:T(8,128)}) fusion(f32[64,256]{1,0:T(8,128)S(1)} %get-tuple-element.37, f32[64,256]{1,0:T(8,128)S(1)} %get-tuple-element.36, f32[16,256]{1,0:T(8,128)S(1)} %get-tuple-element.45, ...), kind=kLoop, calls=%fused_computation.40 | loop fusion | flops 3145728 | bytes 4489216 | tf_op jit(solution)/shard_map/sub | solution.py:29
  10.6 2.6 %copy.47 = f32[1024,256]{0,1:T(8,128)} copy(f32[1024,256]{1,0:T(8,128)} %bitcast.75) | data formatting | bytes 2097152 | tf_op jit(solution)/shard_map/sub | solution.py:29
  13.1 1.3 %copy.48 = f32[1024,256]{0,1:T(8,128)} copy(f32[1024,256]{1,0:T(8,128)S(1)} %bitcast.74) | data formatting | bytes 2097152 | tf_op jit(solution)/shard_map/add | solution.py:29
  15.7 2.7 %subtract_convert_fusion.1 = (bf16[4,1024,256]{1,2,0:T(8,128)(2,1)S(1)}, bf16[4,1024,256]{1,2,0:T(8,128)(2,1)S(1)}) fusion(f32[1024,256]{0,1:T(8,128)} %copy.48, f32[4,1024]{1,0:T(4,128)S(1)} %get-tuple-element.46, f32[1024,256]{0,1:T(8,128)} %copy.47, f32[4,1024]{1,0:T(4,128)S(1)} %get-tuple-element.47), kind=kLoop, calls=%fused_computation.13 | loop fusion | flops 8388608 | bytes 6324224 | tf_op jit(solution)/shard_map/convert_element_type | solution.py:56
  18.5 1.1 %subtract_convert_fusion = (bf16[4,1024,256]{1,2,0:T(8,128)(2,1)S(1)}, bf16[4,1024,256]{1,2,0:T(8,128)(2,1)S(1)}) fusion(f32[1024,256]{0,1:T(8,128)S(1)} %copy.52, f32[4,1024]{1,0:T(4,128)S(1)} %get-tuple-element.31, f32[1024,256]{0,1:T(8,128)S(1)} %copy.51, f32[4,1024]{1,0:T(4,128)S(1)} %get-tuple-element.30), kind=kLoop, calls=%fused_computation.11 | loop fusion | flops 8388608 | bytes 6324224 | tf_op jit(solution)/shard_map/convert_element_type | solution.py:56
  19.6 3.6 %fusion = f32[4,512,512]{2,1,0:T(8,128)S(1)} fusion(bf16[4,1024,256]{1,2,0:T(8,128)(2,1)S(1)} %get-tuple-element.15, bf16[4,1024,256]{1,2,0:T(8,128)(2,1)S(1)} %get-tuple-element.14, bf16[512,1024]{1,0:T(8,128)(2,1)} %fusion.20), kind=kOutput, calls=%fused_computation | convolution fusion | flops 2155872256 | bytes 9437184 | tf_op jit(solution)/shard_map/sra,rb->sab/dot_general | solution.py:76
  23.2 3.6 %fusion.17 = f32[4,512,512]{2,1,0:T(8,128)S(1)} fusion(f32[4,512,512]{2,1,0:T(8,128)S(1)} %fusion, bf16[4,1024,256]{1,2,0:T(8,128)(2,1)S(1)} %get-tuple-element.13, bf16[4,1024,256]{1,2,0:T(8,128)(2,1)S(1)} %get-tuple-element.12, bf16[1024,512]{0,1:T(8,128)(2,1)} %collective-permute-done), kind=kOutput, calls=%fused_computation.27 | convolution fusion | flops 2156920832 | bytes 13631488 | tf_op jit(solution)/shard_map/sra,rb->sab/dot_general | solution.py:76
  26.8 0.5 subtract_convert_fusion.2
  27.3 1.1 %copy_bitcast_fusion = bf16[16,4,2,16,256]{4,3,1,2,0:T(8,128)(2,1)} fusion(bf16[4,1,16,16,256]{4,3,2,0,1:T(8,128)(2,1)S(1)} %bitcast.77, bf16[4,1,16,16,256]{4,3,2,0,1:T(8,128)(2,1)S(1)} %bitcast.76), kind=kLoop, calls=%fused_computation.34 | loop fusion | flops 524288 | bytes 2097152 | tf_op jit(solution)/shard_map/transpose | solution.py:108
  28.4 7.4 %all-to-all-start = ((bf16[16,4,2,16,256]{4,3,1,2,0:T(8,128)(2,1)}), bf16[16,4,2,16,256]{4,3,1,2,0:T(8,128)(2,1)S(1)}, u32[]{:S(2)}, u32[]{:S(2)}) async-start(bf16[16,4,2,16,256]{4,3,1,2,0:T(8,128)(2,1)} %copy_bitcast_fusion), calls=%async_computation | async-start | bytes 2097152 | tf_op jit(solution)/shard_map/all_to_all | solution.py:112
  36.0 2.5 %multiply_convert_fusion.2 = (bf16[256,512]{1,0:T(8,128)(2,1)S(1)}, bf16[256,512]{1,0:T(8,128)(2,1)S(1)}) fusion(s32[512]{0:T(512)S(1)} %iota_add_fusion.3, s32[256]{0:T(256)S(1)} %iota_add_fusion.4), kind=kLoop, calls=%fused_computation.54 | loop fusion | flops 2359296 | bytes 527360 | tf_op jit(solution)/shard_map/convert_element_type | solution.py:63
  38.5 14.5 %all-to-all-done = bf16[16,4,2,16,256]{4,3,1,2,0:T(8,128)(2,1)S(1)} async-done(((bf16[16,4,2,16,256]{4,3,1,2,0:T(8,128)(2,1)}), bf16[16,4,2,16,256]{4,3,1,2,0:T(8,128)(2,1)S(1)}, u32[]{:S(2)}, u32[]{:S(2)}) %all-to-all-start) | async-done | bytes 1048608 | tf_op jit(solution)/shard_map/all_to_all | solution.py:112
  53.4 0.4 stack.26
  54.4 0.6 copy.58
  56.0 30.7 %all_to_all.10 = bf16[128,12,128]{2,1,0:T(8,128)(2,1)S(1)} all-to-all(bf16[128,12,128]{2,1,0:T(8,128)(2,1)S(1)} %reshape.703), channel_id=1, replica_groups=mesh['facet'=128,'half'=2] {'facet'}, dimensions={0} | all-to-all | bytes 786432 | tf_op jit(solution)/shard_map/all_to_all | solution.py:141
  86.7 3.6 %reshape.706 = f32[4,8,4,3,2,16,16]{6,5,4,3,2,1,0:T(8,128)} reshape(bf16[128,12,128]{2,1,0:T(8,128)(2,1)S(1)} %all_to_all.10) | data formatting | bytes 1179648 | tf_op jit(solution)/shard_map/convert_element_type | solution.py:144
  90.3 3.7 %reduce_sum.35 = f32[4,4,3,2,16,16]{5,4,3,2,1,0:T(8,128)S(1)} reduce(f32[4,8,4,3,2,16,16]{6,5,4,3,2,1,0:T(8,128)} %reshape.706, f32[]{:T(128)} %constant.211.clone.1), dimensions={1}, to_apply=%region_2.3 | reduce | flops 172032 | bytes 884740 | tf_op jit(solution)/shard_map/reduce_sum | solution.py:144
  95.0 0.7 maximum_bitcast_fusion.4
  (48 shorter events, 5.2 us)
Async XLA Ops:
  2.4 2.2 %copy-start.3 = (bf16[1,1024,2048]{2,1,0:T(8,128)(2,1)S(1)}, bf16[1,1024,2048]{2,1,0:T(8,128)(2,1)}, u32[]{:S(2)}) copy-start(bf16[1,1024,2048]{2,1,0:T(8,128)(2,1)} %param.5) | copy-start | bytes 12582916
  8.0 15.2 %collective-permute-start = (bf16[1024,512]{0,1:T(8,128)(2,1)}, bf16[1024,512]{0,1:T(8,128)(2,1)}, u32[]{:S(2)}, u32[]{:S(2)}) collective-permute-start(bf16[1024,512]{0,1:T(8,128)(2,1)} %bitcast.13), channel_id=1, source_target_pairs={{0,1},{1,0},{2,3},{3,2},{4,5},{5,4},{6,7},{7,6},{8,9},{9,8},{10,11... | collective-permute-start | bytes 3145736 | tf_op jit(solution)/shard_map/ppermute | solution.py:92
  10.6 4.6 %copy-start = (s32[1,8]{1,0:T(1,128)S(1)}, s32[1,8]{1,0:T(1,128)}, u32[]{:S(2)}) copy-start(s32[1,8]{1,0:T(1,128)} %param.6) | copy-start | bytes 100
  10.6 4.6 %copy-start.1 = (s32[8]{0:T(128)S(1)}, s32[8]{0:T(128)}, u32[]{:S(2)}) copy-start(s32[8]{0:T(128)} %param.7) | copy-start | bytes 100
  26.8 9.0 %copy-start.2 = (s32[2,128]{1,0:T(2,128)S(1)}, s32[2,128]{1,0:T(2,128)}, u32[]{:S(2)}) copy-start(s32[2,128]{1,0:T(2,128)} %param.9) | copy-start | bytes 3076
  28.4 24.5 %all-to-all-start = ((bf16[16,4,2,16,256]{4,3,1,2,0:T(8,128)(2,1)}), bf16[16,4,2,16,256]{4,3,1,2,0:T(8,128)(2,1)S(1)}, u32[]{:S(2)}, u32[]{:S(2)}) async-start(bf16[16,4,2,16,256]{4,3,1,2,0:T(8,128)(2,1)} %copy_bitcast_fusion), calls=%async_computation | async-start | bytes 2097152 | tf_op jit(solution)/shard_map/all_to_all | solution.py:112

commit v2 on v1

v2 whole, which is shorter than its diff:
```python
import functools
import math

import jax
import jax.numpy as jnp
from jax import lax
from jax.experimental import pallas as pl
from jax.experimental.pallas import tpu as pltpu
from jax.sharding import PartitionSpec as P

FS = 2048
M = 256
SG = 512
IMAGE = 131072
SUBGRIDS = 8
CAP = 3
NX, NZ, NY = 4, 8, 4
GROUP = NX * NY
KB = M // GROUP
FINE = 32
SPAN = 512

TWO_PI = 2.0 * math.pi
STRIDE = IMAGE // FS


def unit(product, period):
    quarter = period // 4
    shifted = product + quarter // 2
    turn = jnp.right_shift(shifted, quarter.bit_length() - 1) & 3
    x = ((shifted & (quarter - 1)) - quarter // 2).astype(jnp.float32) * (TWO_PI / period)
    z = x * x
    s = x + x * z * (-1.0 / 6 + z * (1.0 / 120 + z * (-1.0 / 5040 + z * (1.0 / 362880))))
    c = 1.0 + z * (-0.5 + z * (1.0 / 24 + z * (-1.0 / 720 + z * (1.0 / 40320))))
    odd = (turn & 1) == 1
    re = jnp.where(odd, s, c)
    im = jnp.where(odd, c, s)
    return (
        jnp.where((turn == 1) | (turn == 2), -re, re),
        jnp.where(turn >= 2, -im, im),
    )


def cmul(a, b):
    return a[0] * b[0] - a[1] * b[1], a[0] * b[1] + a[1] * b[0]


def taper_of(place):
    relative = place.astype(jnp.float32) * (2.0 / FS)
    return jnp.exp(-2.0 * relative * relative) * (1.0 / math.sqrt(FS))


def fold_kernel(offset_ref, x_hbm, out_ref, big_re, big_im, *scratch):
    steps = FS // SPAN
    images, tables, sem = scratch[:steps], scratch[steps : 2 * steps], scratch[-1]
    copies = [
        pltpu.make_async_copy(x_hbm.at[:, pl.ds(n * SPAN, SPAN)], images[n], sem.at[n])
        for n in range(steps)
    ]
    for copy in copies:
        copy.start()

    def wave(rows, step, start):
        shape = (rows, M)
        place = lax.broadcasted_iota(jnp.int32, shape, 0) * step + start
        tick = (lax.broadcasted_iota(jnp.int32, shape, 1) - M // 2) * STRIDE
        freq = (offset_ref[0] + tick) & (IMAGE - 1)
        return unit(-(place * freq), IMAGE)

    big_re[...], big_im[...] = wave(FS // FINE, FINE, -FS // 2)
    small = wave(FINE, 1, 0)
    row = lax.broadcasted_iota(jnp.int32, (FINE, 128), 0)

    def make(n):
        for m in range(SPAN // FINE):
            at = n * (SPAN // FINE) + m
            big = big_re[at : at + 1, :], big_im[at : at + 1, :]
            taper = taper_of(row + (at * FINE - FS // 2))
            taper = jnp.concatenate([taper, taper], axis=1)
            re, im = cmul(big, small)
            rows = slice(m * FINE, (m + 1) * FINE)
            tables[n][rows, :M] = (taper * re).astype(jnp.bfloat16)
            tables[n][rows, M:] = (taper * im).astype(jnp.bfloat16)

    make(0)
    total = None
    for n in range(steps):
        copies[n].wait()
        if n + 1 < steps:
            make(n + 1)
        term = jnp.dot(
            images[n][...], tables[n][...], preferred_element_type=jnp.float32
        )
        total = term if total is None else total + term
    out_ref[...] = total.astype(jnp.bfloat16)


def fold(pixels, column_offset):
    rows = pixels.shape[0]
    steps = FS // SPAN
    return pl.pallas_call(
        fold_kernel,
        out_shape=jax.ShapeDtypeStruct((rows, 2 * M), jnp.bfloat16),
        in_specs=[
            pl.BlockSpec(memory_space=pltpu.SMEM),
            pl.BlockSpec(memory_space=pl.ANY),
        ],
        out_specs=pl.BlockSpec(memory_space=pltpu.VMEM),
        scratch_shapes=[
            pltpu.VMEM((FS // FINE, M), jnp.float32),
            pltpu.VMEM((FS // FINE, M), jnp.float32),
        ]
        + [pltpu.VMEM((rows, SPAN), jnp.bfloat16)] * steps
        + [pltpu.VMEM((SPAN, 2 * M), jnp.bfloat16)] * steps
        + [pltpu.SemaphoreType.DMA((steps,))],
        cost_estimate=pl.CostEstimate(
            flops=4 * rows * FS * M, bytes_accessed=rows * FS * 2, transcendentals=0
        ),
        compiler_params=pltpu.CompilerParams(vmem_limit_bytes=24 << 20),
        name="fold",
    )(column_offset, pltpu.with_memory_space_constraint(pixels, pltpu.HBM))


def order(n):
    return jnp.where(n < M // 2, n, M // 2 - 1 - n)


def row_kernel(first, *refs):
    half_ref, offset_ref = refs[:2]
    if first:
        f, out_ref, next_re, next_im, wave_re, wave_im, *tables = refs[2:]
    else:
        w_re, w_im, wave_re, wave_im, acc, f, out_ref, *tables = refs[2:]
    count = len(tables) // 2
    rows = f.shape[0]
    start = (half_ref[0] - 1 if first else 0 - half_ref[0]) * rows

    lane = lax.broadcasted_iota(jnp.int32, (8, rows), 1) + start
    taper = taper_of(lane[:1])
    sub = lax.broadcasted_iota(jnp.int32, (8, rows), 0)
    freq = jnp.zeros((8, rows), jnp.int32)
    for n in range(count):
        freq = jnp.where(sub == n, offset_ref[n] - STRIDE // 2, freq)
    gain = unit(-(lane * freq), IMAGE)
    gain = gain[0] * taper, gain[1] * taper

    wide = 128
    if first:
        shape = (M // 2, wide)
        odd = 2 * lax.broadcasted_iota(jnp.int32, shape, 0) + 1
        place = lax.broadcasted_iota(jnp.int32, shape, 1) + start
        blocks = [unit(-(odd * place), 2 * FS)]
        step = unit(-(odd * wide), 2 * FS)
        while len(blocks) < rows // wide:
            blocks += [cmul(block, step) for block in blocks]
            step = cmul(step, step)
        sign = (2 - (odd & 3)) * (2 * half_ref[0] - 1)
        sign = sign.astype(jnp.float32)
        for n, block in enumerate(blocks):
            at = slice(n * wide, (n + 1) * wide)
            wave_re[:, at], wave_im[:, at] = block
            next_re[:, at], next_im[:, at] = -sign * block[1], sign * block[0]

    def make(n):
        re, im = tables[2 * n], tables[2 * n + 1]
        for m in range(rows // wide):
            at = slice(m * wide, (m + 1) * wide)
            g = gain[0][n : n + 1, at], gain[1][n : n + 1, at]
            d = wave_re[:, at], wave_im[:, at]
            rr, ii, ri, ir = g[0] * d[0], g[1] * d[1], g[0] * d[1], g[1] * d[0]
            re[: M // 2, at] = (rr - ii).astype(jnp.bfloat16)
            im[: M // 2, at] = (ri + ir).astype(jnp.bfloat16)
            re[M // 2 :, at] = (rr + ii).astype(jnp.bfloat16)
            im[M // 2 :, at] = (ir - ri).astype(jnp.bfloat16)

    make(0)
    for n in range(count):
        if n + 1 < count:
            make(n + 1)
        by_re, by_im = (
            jnp.dot(t[...], f[...], preferred_element_type=jnp.float32)
            for t in tables[2 * n : 2 * n + 2]
        )
        part = by_re[:, :M] - by_im[:, M:], by_re[:, M:] + by_im[:, :M]
        if first:
            out_ref[n, 0], out_ref[n, 1] = part
        else:
            part = part[0] + acc[n, 0], part[1] + acc[n, 1]
            y = cmul((w_re[n], w_im[n]), part)
            for c in range(2):
                out_ref[:, n, c] = y[c].astype(jnp.bfloat16).reshape(GROUP, KB, M)


def row_product(half, offsets, weight, mine, swap):
    rows = mine.shape[0]
    count = offsets.shape[0]
    smem = pl.BlockSpec(memory_space=pltpu.SMEM)
    vmem = pl.BlockSpec(memory_space=pltpu.VMEM)
    wave = jax.ShapeDtypeStruct((M // 2, rows), jnp.float32)
    tables = [pltpu.VMEM((M, rows), jnp.bfloat16)] * (2 * count)
    cost = pl.CostEstimate(
        flops=8 * count * rows * M * M, bytes_accessed=4 << 20, transcendentals=0
    )
    params = pltpu.CompilerParams(vmem_limit_bytes=24 << 20)
    half = half.reshape(1)
    acc, next_re, next_im = pl.pallas_call(
        functools.partial(row_kernel, True),
        out_shape=(jax.ShapeDtypeStruct((count, 2, M, M), jnp.float32), wave, wave),
        in_specs=[smem, smem, vmem],
        out_specs=(vmem, vmem, vmem),
        scratch_shapes=[pltpu.VMEM(wave.shape, wave.dtype)] * 2 + tables,
        cost_estimate=cost,
        compiler_params=params,
        name="row_mine",
    )(half, offsets, mine)
    other = swap()
    return pl.pallas_call(
        functools.partial(row_kernel, False),
        out_shape=jax.ShapeDtypeStruct((GROUP, count, 2, KB, M), jnp.bfloat16),
        in_specs=[smem] * 4 + [vmem] * 4,
        out_specs=vmem,
        scratch_shapes=tables,
        cost_estimate=cost,
        compiler_params=params,
        name="row_other",
    )(half, offsets, *weight, next_re, next_im, acc, other)


def grid_table(ticks_in):
    ticks_out = jnp.arange(SG, dtype=jnp.int32) - SG // 2
    grid = unit(ticks_in[:, None] * ticks_out[None, :], SG)
    return [(g * (1.0 / math.sqrt(M))).astype(jnp.bfloat16) for g in grid]


def facet_weight(facet_id, offsets, column, cover):
    ratio = STRIDE
    shift_a = (7 * facet_id) % ratio - ratio // 2
    shift_b = (5 * (facet_id // ratio) + 3 * facet_id) % ratio - ratio // 2
    turn = shift_a * ((FS * offsets) & (IMAGE - 1)) + shift_b * ((FS * column) & (IMAGE - 1))
    w = unit(-turn, IMAGE)
    return cover * w[0], cover * w[1]


def dot(spec, a, b):
    return jnp.einsum(spec, a, b, preferred_element_type=jnp.float32)


def shards(facet_image, coverage, row_offsets, column_offset, piece_owner):
    half = lax.axis_index("half")
    facet_id = lax.axis_index("facet")
    per_half = SUBGRIDS // 2
    offsets = lax.dynamic_slice_in_dim(row_offsets, half * per_half, per_half, 0)
    cover = lax.dynamic_slice_in_dim(coverage[0], half * per_half, per_half, 0)

    folded = fold(facet_image[0], column_offset)
    weight = facet_weight(facet_id, offsets, column_offset[0], cover.astype(jnp.float32))
    y = row_product(
        half,
        offsets,
        weight,
        folded,
        lambda: lax.ppermute(folded, "half", [(0, 1), (1, 0)]),
    )
    groups = [
        [(x * NZ + z) * NY + v for x in range(NX) for v in range(NY)] for z in range(NZ)
    ]
    y = lax.all_to_all(
        y, "facet", split_axis=0, concat_axis=0, axis_index_groups=groups, tiled=True
    )
    y = jnp.sum(y, axis=0, dtype=jnp.float32).astype(jnp.bfloat16)

    ticks = jnp.arange(M, dtype=jnp.int32)
    wide = jnp.concatenate(grid_table(ticks - M // 2), axis=1)
    wide_out = jnp.concatenate(grid_table(order(ticks)), axis=1)
    full = dot("sckl,lj->sckj", y, wide)
    spread = jnp.stack(
        [
            full[:, 0, :, :SG] - full[:, 1, :, SG:],
            full[:, 0, :, SG:] + full[:, 1, :, :SG],
        ],
        axis=1,
    ).astype(jnp.bfloat16)
    width = 16
    blocks_per = SG // width
    pieces = spread.reshape(per_half, 2, KB, blocks_per, width)
    pieces = pieces.transpose(0, 3, 1, 2, 4).reshape(per_half * blocks_per, 2 * KB * width)

    owners = lax.dynamic_index_in_dim(piece_owner, half, 0, keepdims=False)
    count = owners.shape[0]
    place = jnp.arange(count, dtype=jnp.int32)
    same = (owners[:, None] == owners[None, :]) & (place[:, None] < place[None, :])
    slot_of = jnp.sum(same.astype(jnp.int32), axis=0)
    target = jnp.arange(count * CAP, dtype=jnp.int32)
    pick = (target[:, None] == (owners * CAP + slot_of)[None, :]).astype(jnp.bfloat16)
    outbox = jnp.dot(pick, pieces, preferred_element_type=jnp.float32)
    outbox = outbox.astype(jnp.bfloat16).reshape(count, CAP, 2 * KB * width // 128, 128)
    inbox = lax.all_to_all(outbox, "facet", split_axis=0, concat_axis=0, tiled=True)

    inbox = inbox.reshape(NX, NZ, NY, CAP, 2 * KB * width // 128, 128)
    summed = jnp.sum(inbox, axis=1, dtype=jnp.float32) * (1.0 / math.sqrt(count))
    summed = lax.optimization_barrier(summed.astype(jnp.bfloat16))
    summed = summed.reshape(NX, NY, CAP, 2, KB, width).transpose(2, 3, 5, 0, 1, 4)
    summed = summed.reshape(CAP, 2, width, M)
    out = dot("cdjk,ki->cdji", summed, wide_out)
    out_re = out[:, 0, :, :SG] - out[:, 1, :, SG:]
    out_im = out[:, 0, :, SG:] + out[:, 1, :, :SG]
    return jnp.stack([out_re, out_im], axis=1)[None, None]


def solution(mesh):
    return jax.shard_map(
        shards,
        mesh=mesh,
        in_specs=(P("facet", "half", None), P("facet", None), P(), P(), P()),
        out_specs=P("half", "facet", None, None, None, None),
        check_vma=False,
    )
```

time: 96.1 us -> 71 us (0.74)
  other arithmetic: 18.3 us -> 3.23 us
  Pallas kernels: 0 us -> 12.1 us
  matrix products: 11.3 us -> 0.72 us
  local copies, waits for them, and re-layouts: 12.6 us -> 2.8 us
  blocking collectives: 30.7 us -> 28.1 us
    pallas_call x0 -> x3, Pallas kernels: none -> 12.1 us  [the longest x1 4.42 us: fold(): pl.pallas_call(fold_kernel, out_shape=jax.ShapeDtypeStruct((rows, 2 * M),...]
    dot_general x4 -> x2, matrix products: 7.66 us -> 0.45 us  [dot(): return jnp.einsum(spec, a, b, preferred_element_type=jnp.float32)]
    convert_element_type x5 -> x2, other arithmetic: 7.39 us -> 1.57 us  [the longest x1 1.54 us: grid_table(): return [(g * (1.0 / math.sqrt(M))).astype(jnp.bfloat16) for g in grid]]
    convert_element_type x2 -> x0, local copies, waits for them, and re-layouts: 3.95 us -> none  [the longest x1 3.59 us: shards(): jnp.sum(inbox, axis=1, dtype=jnp.float32) * (1.0 / math.sqrt(count))]
    reduce_sum x1, other arithmetic: 3.67 us -> 0.17 us  [shards(): jnp.sum(inbox, axis=1, dtype=jnp.float32) * (1.0 / math.sqrt(count))]
    dot_general x1 -> x0, matrix products: 3.37 us -> none  [shards(): jnp.dot(pixels, col, preferred_element_type=jnp.float32)]
    sub x2 -> x0, local copies, waits for them, and re-layouts: 2.88 us -> none  [cmul(): return (a[0] * b[0] - a[1] * b[1], a[0] * b[1] + a[1] * b[0])]
    all_to_all x1, blocking collectives: 30.7 us -> 28.1 us  [shards(): lax.all_to_all(outbox, 'facet', split_axis=0, concat_axis=0, tiled=True)]
  transfers between devices with their start and end apart: 2 -> 2, of which waited for: 1 -> 1; matrix products, arithmetic and copies ran while one was open for 18% -> 3% of each run, Pallas kernels for 0% -> 5%
where the time goes in v2:
time: 71 us; the launch traced here: 70.7 us
  blocking collectives  28.1 us (40%)
  waiting for transfers between devices  15.3 us (22%)
  Pallas kernels  12.1 us (17%)
  starting transfers between devices  7.48 us (11%)
  other arithmetic  3.23 us (5%)
  local copies, waits for them, and re-layouts  2.8 us (4%)
  between operations  0.91 us (1%)
  matrix products  0.72 us (1%)
    all_to_all x1, blocking collectives, shards(): lax.all_to_all(outbox, 'facet', split_axis=0, concat_axis=0, tiled=True)  28.1 us
    all_to_all x1, waiting for transfers between devices, shards(): lax.all_to_all(y, 'facet', split_axis=0, concat_axis=0, axis_index_groups...  15.3 us
    all_to_all x1, starting transfers between devices, shards(): lax.all_to_all(y, 'facet', split_axis=0, concat_axis=0, axis_index_groups...  7.39 us
    pallas_call x1, Pallas kernels, fold(): pl.pallas_call(fold_kernel, out_shape=jax.ShapeDtypeStruct((rows, 2 * M),...  4.42 us
    pallas_call x1, Pallas kernels, row_product(): pl.pallas_call(functools.partial(row_kernel, False), out_shape=jax.ShapeD...  4.4 us
    pallas_call x1, Pallas kernels, row_product(): pl.pallas_call(functools.partial(row_kernel, True), out_shape=(jax.ShapeD...  3.28 us
    convert_element_type x1, other arithmetic, grid_table(): return [(g * (1.0 / math.sqrt(M))).astype(jnp.bfloat16) for g in grid]  1.54 us
  transfers between devices with their start and end apart: 2, of which 1 were waited for; matrix products, arithmetic and copies ran while one was open for 3% of the time, Pallas kernels for 5%

profile of v2, /device:TPU:8, one launch (start us, length us, event | category | flops | bytes accessed | tf_op | source)
XLA Modules:
  0.0 70.7 jit_solution(8536518486778200209)
XLA Ops:
  0.7 4.4 %fold.1.refs_2_ = bf16[1024,512]{1,0:T(8,128)(2,1)S(1)} custom-call(s32[1]{0:T(128)S(6)} %copy.13.offset_ref, bf16[1024,2048]{1,0:T(8,128)(2,1)} %bitcast.42), custom_call_target="tpu_custom_call" | custom-call | flops 2147483648 | bytes 4194304 | tf_op jit(solution)/shard_map/fold/pallas_call | solution.py:101
  5.3 0.1 bitcast_multiply_fusion
  5.4 3.3 %row_mine.1 = (f32[4,2,256,256]{3,2,1,0:T(8,128)S(1)}, f32[128,1024]{1,0:T(8,128)S(1)}, f32[128,1024]{1,0:T(8,128)S(1)}) custom-call(s32[1]{0:T(128)} %bitcast.3.refs_0_, s32[4]{0:T(128)S(1)} %get-tuple-element.13.refs_1_, bf16[1024,512]{1,0:T(8,128)(2,1)S(1)} %fold.1.refs_2_), custom_call_target="tpu_custom_call" | custom-call | flops 2147483648 | bytes 4194304 | tf_op jit(solution)/shard_map/row_mine/pallas_call | solution.py:206
  8.8 4.4 %row_other.1 = bf16[16,4,2,16,256]{4,3,2,1,0:T(8,128)(2,1)} custom-call(s32[1]{0:T(128)} %bitcast.3.refs_0_, s32[4]{0:T(128)S(1)} %get-tuple-element.13.refs_1_, f32[4]{0:T(128)S(1)} %bitcast_multiply_fusion.1.refs_2_, f32[4]{0:T(128)S(1)} %get-tuple-element.11.refs_3_, f32[128,1024]{1,0:T(8,128)S(1)} %get-tuple-element.8.refs_4_, ...), custom_call_target="tpu_custom_call" | custom-call | flops 2147483648 | bytes 4194304 | tf_op jit(solution)/shard_map/row_other/pallas_call | solution.py:217
  13.2 7.4 %all-to-all-start = ((bf16[16,4,2,16,256]{4,3,2,1,0:T(8,128)(2,1)}), bf16[16,4,2,16,256]{4,3,2,1,0:T(8,128)(2,1)S(1)}, u32[]{:S(2)}, u32[]{:S(2)}) async-start(bf16[16,4,2,16,256]{4,3,2,1,0:T(8,128)(2,1)} %row_other.1), calls=%async_computation | async-start | bytes 2097152 | tf_op jit(solution)/shard_map/all_to_all | solution.py:267
  20.6 0.1 convert_reduce_fusion.1
  20.7 1.5 %fusion.23 = (bf16[256,512]{1,0:T(8,128)(2,1)S(1)}, bf16[256,512]{1,0:T(8,128)(2,1)S(1)}, bf16[256,512]{1,0:T(8,128)(2,1)S(1)}, bf16[256,512]{1,0:T(8,128)(2,1)S(1)}) fusion(s32[256]{0:T(256)S(1)} %get-tuple-element.24, s32[512]{0:T(512)S(1)} %iota_add_fusion, s32[256]{0:T(256)S(1)} %get-tuple-element.25), kind=kLoop, calls=%fused_computation.46 | loop fusion | flops 11010048 | bytes 1052672 | tf_op jit(solution)/shard_map/convert_element_type | solution.py:232
  22.2 15.3 %all-to-all-done = bf16[16,4,2,16,256]{4,3,2,1,0:T(8,128)(2,1)S(1)} async-done(((bf16[16,4,2,16,256]{4,3,2,1,0:T(8,128)(2,1)}), bf16[16,4,2,16,256]{4,3,2,1,0:T(8,128)(2,1)S(1)}, u32[]{:S(2)}, u32[]{:S(2)}) %all-to-all-start) | async-done | bytes 1048608 | tf_op jit(solution)/shard_map/all_to_all | solution.py:267
  37.6 0.2 reduce_sum.34
  37.8 0.2 fusion.26
  38.1 0.4 stack.14
  38.5 0.4 stack.15
  38.8 0.2 maximum_bitcast_fusion
  39.1 0.6 copy.9
  39.7 0.3 reshape.49
  40.0 0.3 convolution_convert_fusion
  40.3 0.1 reshape.50
  40.4 28.1 %all_to_all.10 = bf16[128,3,4,128]{3,2,1,0:T(4,128)(2,1)S(1)} all-to-all(bf16[128,3,4,128]{3,2,1,0:T(4,128)(2,1)S(1)} %reshape.50), channel_id=1, replica_groups=mesh['facet'=128,'half'=2] {'facet'}, dimensions={0} | all-to-all | bytes 786432 | tf_op jit(solution)/shard_map/all_to_all | solution.py:297
  68.5 0.2 convert_reduce_fusion
  68.7 0.3 reshape.51
  69.0 0.4 copy.10
  69.4 0.3 reshape.52
  69.7 0.2 fusion.29
  70.0 0.7 maximum_bitcast_fusion.5
  (16 shorter events, 0.3 us)
Async XLA Ops:
  0.0 5.3 %copy-start = (s32[1,8]{1,0:T(1,128)S(1)}, s32[1,8]{1,0:T(1,128)}, u32[]{:S(2)}) copy-start(s32[1,8]{1,0:T(1,128)} %param.6) | copy-start | bytes 100
  0.0 5.3 %copy-start.1 = (s32[8]{0:T(128)S(1)}, s32[8]{0:T(128)}, u32[]{:S(2)}) copy-start(s32[8]{0:T(128)} %param.7) | copy-start | bytes 100
  5.1 3.6 %collective-permute-start = (bf16[1024,512]{1,0:T(8,128)(2,1)S(1)}, bf16[1024,512]{1,0:T(8,128)(2,1)S(1)}, u32[]{:S(2)}, u32[]{:S(2)}) collective-permute-start(bf16[1024,512]{1,0:T(8,128)(2,1)S(1)} %fold.1.refs_2_), channel_id=1, source_target_pairs={{0,1},{1,0},{2,3},{3,2},{4,5},{5,4},{6,7},{7,6},{8,9},{9,8},{10,11... | collective-permute-start | bytes 3145736 | tf_op jit(solution)/shard_map/ppermute | solution.py:262
  8.8 11.8 %copy-start.2 = (s32[2,128]{1,0:T(2,128)S(1)}, s32[2,128]{1,0:T(2,128)}, u32[]{:S(2)}) copy-start(s32[2,128]{1,0:T(2,128)} %param.9) | copy-start | bytes 3076
  13.2 24.4 %all-to-all-start = ((bf16[16,4,2,16,256]{4,3,2,1,0:T(8,128)(2,1)}), bf16[16,4,2,16,256]{4,3,2,1,0:T(8,128)(2,1)S(1)}, u32[]{:S(2)}, u32[]{:S(2)}) async-start(bf16[16,4,2,16,256]{4,3,2,1,0:T(8,128)(2,1)} %row_other.1), calls=%async_computation | async-start | bytes 2097152 | tf_op jit(solution)/shard_map/all_to_all | solution.py:267

commit v3 on v2

--- a/solution.py
+++ b/solution.py
@@ -19,6 +19,7 @@
 KB = M // GROUP
 FINE = 32
 SPAN = 512
+WIDTH = 16
 
 TWO_PI = 2.0 * math.pi
 STRIDE = IMAGE // FS
@@ -130,7 +131,9 @@
     if first:
         f, out_ref, next_re, next_im, wave_re, wave_im, *tables = refs[2:]
     else:
-        w_re, w_im, wave_re, wave_im, acc, f, out_ref, *tables = refs[2:]
+        w_re, w_im, wave_re, wave_im, acc, f, out_ref, zero, box, sem, *tables = refs[2:]
+        zero[...] = jnp.zeros_like(zero)
+        copies = []
     count = len(tables) // 2
     rows = f.shape[0]
     start = (half_ref[0] - 1 if first else 0 - half_ref[0]) * rows
@@ -188,7 +191,12 @@
             part = part[0] + acc[n, 0], part[1] + acc[n, 1]
             y = cmul((w_re[n], w_im[n]), part)
             for c in range(2):
-                out_ref[:, n, c] = y[c].astype(jnp.bfloat16).reshape(GROUP, KB, M)
+                box[n, :, c] = y[c].astype(jnp.bfloat16).reshape(GROUP, KB, M)
+            copies.append(pltpu.make_async_copy(box.at[n], out_ref.at[:, n], sem.at[n]))
+            copies[n].start()
+    if not first:
+        for copy in copies:
+            copy.wait()
 
 
 def row_product(half, offsets, weight, mine, swap):
@@ -216,20 +224,129 @@
     other = swap()
     return pl.pallas_call(
         functools.partial(row_kernel, False),
-        out_shape=jax.ShapeDtypeStruct((GROUP, count, 2, KB, M), jnp.bfloat16),
+        out_shape=(
+            jax.ShapeDtypeStruct((GROUP, count, 2, KB, M), jnp.bfloat16),
+            jax.ShapeDtypeStruct((1, 128), jnp.int32),
+        ),
         in_specs=[smem] * 4 + [vmem] * 4,
-        out_specs=vmem,
-        scratch_shapes=tables,
+        out_specs=(pl.BlockSpec(memory_space=pltpu.HBM), vmem),
+        scratch_shapes=[
+            pltpu.VMEM((count, GROUP, 2, KB, M), jnp.bfloat16),
+            pltpu.SemaphoreType.DMA((count,)),
+        ]
+        + tables,
         cost_estimate=cost,
         compiler_params=params,
         name="row_other",
     )(half, offsets, *weight, next_re, next_im, acc, other)
 
 
-def grid_table(ticks_in):
-    ticks_out = jnp.arange(SG, dtype=jnp.int32) - SG // 2
-    grid = unit(ticks_in[:, None] * ticks_out[None, :], SG)
-    return [(g * (1.0 / math.sqrt(M))).astype(jnp.bfloat16) for g in grid]
+def grid(tick_in, tick_out):
+    wave = unit(tick_in * tick_out, SG)
+    return [g * (1.0 / math.sqrt(M)) for g in wave]
+
+
+def spread_table(zero):
+    shape = (SG, 2 * M)
+    tick_out = lax.broadcasted_iota(jnp.int32, shape, 0) - SG // 2
+    spot = lax.broadcasted_iota(jnp.int32, shape, 1) + jnp.tile(zero, (1, shape[1] // 128))
+    re, im = grid((spot & (M - 1)) - M // 2, tick_out)
+    return jnp.where(spot < M, re, im).astype(jnp.bfloat16)
+
+
+def finish_table(zero):
+    shape = (2 * M, 2 * SG)
+    row = lax.broadcasted_iota(jnp.int32, shape, 0)
+    spot = lax.broadcasted_iota(jnp.int32, shape, 1) + jnp.tile(zero, (1, shape[1] // 128))
+    tick_in = order(row // (2 * KB) * KB + row % KB)
+    re, im = grid(tick_in, (spot & (SG - 1)) - SG // 2)
+    part = (row // KB) & 1
+    same = part == spot // SG
+    table = jnp.where(same, re, jnp.where(part == 1, -im, im))
+    return table.astype(jnp.bfloat16)
+
+
+def shuffle(rows, start):
+    lane = lax.broadcasted_iota(jnp.int32, rows[0].shape, 1)
+    chunk = 128 // len(rows)
+    out = None
+    for n, row in enumerate(rows):
+        shift = (n - start) * chunk % 128
+        row = pltpu.roll(row, shift, 1) if shift else row
+        out = row if out is None else jnp.where(lane < n * chunk, out, row)
+    return out
+
+
+def spread_kernel(y_ref, grid_ref, pick_ref, out_ref, full, pieces):
+    total = y_ref[0].astype(jnp.float32)
+    for n in range(1, GROUP):
+        total = total + y_ref[n].astype(jnp.float32)
+    turned = []
+    for n in range(0, total.shape[0], 2 * KB):
+        turned += [-total[n + KB : n + 2 * KB], total[n : n + KB]]
+    both = jnp.concatenate([total, jnp.concatenate(turned, axis=0)], axis=1)
+    full[...] = lax.dot_general(
+        grid_ref[...],
+        both.astype(jnp.bfloat16),
+        (((1,), (1,)), ((), ())),
+        preferred_element_type=jnp.float32,
+    )
+    blocks = SG // WIDTH
+    for t in range(WIDTH // 4):
+        rows = [full[pl.ds(4 * q + t, blocks, stride=WIDTH), :] for q in range(4)]
+        for n in range(4):
+            part = shuffle(rows, n).astype(jnp.bfloat16)
+            pieces[n * blocks : (n + 1) * blocks, t * 128 : (t + 1) * 128] = part
+    out_ref[...] = jnp.dot(
+        pick_ref[...], pieces[...], preferred_element_type=jnp.float32
+    ).astype(jnp.bfloat16)
+
+
+def spread(y, table, pick):
+    vmem = pl.BlockSpec(memory_space=pltpu.VMEM)
+    return pl.pallas_call(
+        spread_kernel,
+        out_shape=jax.ShapeDtypeStruct((pick.shape[0], 512), jnp.bfloat16),
+        in_specs=[vmem] * 3,
+        out_specs=vmem,
+        scratch_shapes=[
+            pltpu.VMEM((SG, 128), jnp.float32),
+            pltpu.VMEM((128, 512), jnp.bfloat16),
+        ],
+        compiler_params=pltpu.CompilerParams(vmem_limit_bytes=16 << 20),
+        name="spread",
+    )(y.reshape(GROUP, 128, M), table, pick)
+
+
+def finish_kernel(scale, sum_ref, table_ref, out_ref, rows):
+    rows[...] = jnp.zeros_like(rows)
+    count = sum_ref.shape[1]
+    for q in range(4):
+        for g in range(GROUP // 4):
+            part = shuffle([sum_ref[4 * g + r] * scale for r in range(4)], q)
+            at = slice(g * 128, (g + 1) * 128)
+            rows[q * 16 : q * 16 + count, at] = part.astype(jnp.bfloat16)
+    out = jnp.dot(rows[...], table_ref[...], preferred_element_type=jnp.float32)
+    for q in range(4):
+        for c in range(CAP):
+            at = q * 16 + c * 4
+            for d in range(2):
+                out_ref[c, d, 4 * q : 4 * q + 4, :] = out[
+                    at : at + 4, d * SG : (d + 1) * SG
+                ]
+
+
+def finish(total, table, scale):
+    vmem = pl.BlockSpec(memory_space=pltpu.VMEM)
+    return pl.pallas_call(
+        functools.partial(finish_kernel, scale),
+        out_shape=jax.ShapeDtypeStruct((CAP, 2, WIDTH, SG), jnp.float32),
+        in_specs=[vmem] * 2,
+        out_specs=vmem,
+        scratch_shapes=[pltpu.VMEM((64, 2 * M), jnp.bfloat16)],
+        compiler_params=pltpu.CompilerParams(vmem_limit_bytes=16 << 20),
+        name="finish",
+    )(total, table)
 
 
 def facet_weight(facet_id, offsets, column, cover):
@@ -241,10 +358,6 @@
     return cover * w[0], cover * w[1]
 
 
-def dot(spec, a, b):
-    return jnp.einsum(spec, a, b, preferred_element_type=jnp.float32)
-
-
 def shards(facet_image, coverage, row_offsets, column_offset, piece_owner):
     half = lax.axis_index("half")
     facet_id = lax.axis_index("facet")
@@ -254,7 +367,7 @@
 
     folded = fold(facet_image[0], column_offset)
     weight = facet_weight(facet_id, offsets, column_offset[0], cover.astype(jnp.float32))
-    y = row_product(
+    y, zero = row_product(
         half,
         offsets,
         weight,
@@ -267,44 +380,22 @@
     y = lax.all_to_all(
         y, "facet", split_axis=0, concat_axis=0, axis_index_groups=groups, tiled=True
     )
-    y = jnp.sum(y, axis=0, dtype=jnp.float32).astype(jnp.bfloat16)
-
-    ticks = jnp.arange(M, dtype=jnp.int32)
-    wide = jnp.concatenate(grid_table(ticks - M // 2), axis=1)
-    wide_out = jnp.concatenate(grid_table(order(ticks)), axis=1)
-    full = dot("sckl,lj->sckj", y, wide)
-    spread = jnp.stack(
-        [
-            full[:, 0, :, :SG] - full[:, 1, :, SG:],
-            full[:, 0, :, SG:] + full[:, 1, :, :SG],
-        ],
-        axis=1,
-    ).astype(jnp.bfloat16)
-    width = 16
-    blocks_per = SG // width
-    pieces = spread.reshape(per_half, 2, KB, blocks_per, width)
-    pieces = pieces.transpose(0, 3, 1, 2, 4).reshape(per_half * blocks_per, 2 * KB * width)
-
-    owners = lax.dynamic_index_in_dim(piece_owner, half, 0, keepdims=False)
+
+    owners = lax.dynamic_index_in_dim(piece_owner, half, 0, keepdims=False) + zero[0]
     count = owners.shape[0]
     place = jnp.arange(count, dtype=jnp.int32)
     same = (owners[:, None] == owners[None, :]) & (place[:, None] < place[None, :])
     slot_of = jnp.sum(same.astype(jnp.int32), axis=0)
     target = jnp.arange(count * CAP, dtype=jnp.int32)
     pick = (target[:, None] == (owners * CAP + slot_of)[None, :]).astype(jnp.bfloat16)
-    outbox = jnp.dot(pick, pieces, preferred_element_type=jnp.float32)
-    outbox = outbox.astype(jnp.bfloat16).reshape(count, CAP, 2 * KB * width // 128, 128)
+    pick, last = lax.optimization_barrier((pick, finish_table(zero)))
+    outbox = spread(y, spread_table(zero), pick).reshape(count, CAP, 4, 128)
     inbox = lax.all_to_all(outbox, "facet", split_axis=0, concat_axis=0, tiled=True)
 
-    inbox = inbox.reshape(NX, NZ, NY, CAP, 2 * KB * width // 128, 128)
-    summed = jnp.sum(inbox, axis=1, dtype=jnp.float32) * (1.0 / math.sqrt(count))
-    summed = lax.optimization_barrier(summed.astype(jnp.bfloat16))
-    summed = summed.reshape(NX, NY, CAP, 2, KB, width).transpose(2, 3, 5, 0, 1, 4)
-    summed = summed.reshape(CAP, 2, width, M)
-    out = dot("cdjk,ki->cdji", summed, wide_out)
-    out_re = out[:, 0, :, :SG] - out[:, 1, :, SG:]
-    out_im = out[:, 0, :, SG:] + out[:, 1, :, :SG]
-    return jnp.stack([out_re, out_im], axis=1)[None, None]
+    total = jnp.sum(
+        inbox.reshape(NX, NZ, NY, CAP, 4, 128), axis=1, dtype=jnp.float32
+    ).reshape(GROUP, CAP * 4, 128)
+    return finish(total, last, 1.0 / math.sqrt(count))[None, None]
 
 
 def solution(mesh):

time: 71 us -> 68.4 us (0.963)
  waiting for transfers between devices: 15.3 us -> 10.2 us
  other arithmetic: 3.23 us -> 7.32 us
  local copies, waits for them, and re-layouts: 2.8 us -> 0.17 us
  Pallas kernels: 12.1 us -> 13.9 us
  matrix products: 0.72 us -> 0 us
    convert_element_type x2 -> x3, other arithmetic: 1.57 us -> 6.77 us  [the longest x1 5.19 us: finish_table(): return table.astype(jnp.bfloat16)]
    all_to_all x1, waiting for transfers between devices: 15.3 us -> 10.2 us  [shards(): lax.all_to_all(y, 'facet', split_axis=0, concat_axis=0, axis_index_groups...]
    pallas_call x1 -> x3, Pallas kernels: 4.4 us -> 6.16 us  [the longest x1 4.19 us: row_product(): pl.pallas_call(functools.partial(row_kernel, False), out_shape=(jax.Shape...]
    transpose x2 -> x0, local copies, waits for them, and re-layouts: 1 us -> none  [the longest x1 0.64 us: shards(): pieces.transpose(0, 3, 1, 2, 4)]
    reshape x4 -> x2, local copies, waits for them, and re-layouts: 1 us -> 0.13 us  [the longest x1 0.09 us: shards(): outbox = spread(y, spread_table(zero), pick).reshape(count, CAP, 4, 128)]
    another operation x2 -> x0, local copies, waits for them, and re-layouts: 0.78 us -> none  [shards(): jnp.stack([full[:, 0, :, :SG] - full[:, 1, :, SG:], full[:, 0, :, SG:] +...]
    dot_general x3 -> x0, matrix products: 0.72 us -> none  [the longest x2 0.45 us: dot(): return jnp.einsum(spec, a, b, preferred_element_type=jnp.float32)]
  transfers between devices with their start and end apart: 2 -> 2, of which waited for: 1 -> 1; matrix products, arithmetic and copies ran while one was open for 3% -> 10% of each run, Pallas kernels for 5% -> 5%
where the time goes in v3:
time: 68.4 us; the launch traced here: 68.1 us
  blocking collectives  28.1 us (41%)
  Pallas kernels  13.9 us (20%)
  waiting for transfers between devices  10.2 us (15%)
  starting transfers between devices  7.5 us (11%)
  other arithmetic  7.32 us (11%)
  between operations  0.9 us (1%)
    all_to_all x1, blocking collectives, shards(): lax.all_to_all(outbox, 'facet', split_axis=0, concat_axis=0, tiled=True)  28.1 us
    all_to_all x1, waiting for transfers between devices, shards(): lax.all_to_all(y, 'facet', split_axis=0, concat_axis=0, axis_index_groups...  10.2 us
    all_to_all x1, starting transfers between devices, shards(): lax.all_to_all(y, 'facet', split_axis=0, concat_axis=0, axis_index_groups...  7.41 us
    convert_element_type x1, other arithmetic, finish_table(): return table.astype(jnp.bfloat16)  5.19 us
    pallas_call x1, Pallas kernels, fold(): pl.pallas_call(fold_kernel, out_shape=jax.ShapeDtypeStruct((rows, 2 * M),...  4.44 us
    pallas_call x1, Pallas kernels, row_product(): pl.pallas_call(functools.partial(row_kernel, False), out_shape=(jax.Shape...  4.19 us
    pallas_call x1, Pallas kernels, row_product(): pl.pallas_call(functools.partial(row_kernel, True), out_shape=(jax.ShapeD...  3.28 us
    convert_element_type x1, other arithmetic, spread_table(): return jnp.where(spot < M, re, im).astype(jnp.bfloat16)  1.54 us
  transfers between devices with their start and end apart: 2, of which 1 were waited for; matrix products, arithmetic and copies ran while one was open for 10% of the time, Pallas kernels for 5%

profile of v3, /device:TPU:8, one launch (start us, length us, event | category | flops | bytes accessed | tf_op | source)
XLA Modules:
  0.0 68.1 jit_solution(2742152983037123491)
XLA Ops:
  0.7 0.0 copy-start.1
  0.7 0.0 copy-start.2
  0.7 4.4 %fold.1.refs_2_ = bf16[1024,512]{1,0:T(8,128)(2,1)S(1)} custom-call(s32[1]{0:T(128)S(6)} %copy.11.offset_ref, bf16[1024,2048]{1,0:T(8,128)(2,1)} %bitcast.60), custom_call_target="tpu_custom_call" | custom-call | flops 2147483648 | bytes 4194304 | tf_op jit(solution)/shard_map/fold/pallas_call | solution.py:102
  5.1 0.1 collective-permute-start
  5.3 0.0 copy-done.1
  5.3 0.0 copy-done.2
  5.3 0.1 bitcast_multiply_fusion
  5.4 3.3 %row_mine.1 = (f32[4,2,256,256]{3,2,1,0:T(8,128)S(1)}, f32[128,1024]{1,0:T(8,128)S(1)}, f32[128,1024]{1,0:T(8,128)S(1)}) custom-call(s32[1]{0:T(128)} %bitcast.refs_0_, s32[4]{0:T(128)S(1)} %get-tuple-element.21.refs_1_, bf16[1024,512]{1,0:T(8,128)(2,1)S(1)} %fold.1.refs_2_), custom_call_target="tpu_custom_call" | custom-call | flops 2147483648 | bytes 4194304 | tf_op jit(solution)/shard_map/row_mine/pallas_call | solution.py:214
  8.7 0.1 bitcast_multiply_fusion.1.refs_2_
  8.8 0.0 collective-permute-done.refs_7_
  8.8 0.0 copy-start
  8.8 4.2 %row_other.1 = (bf16[16,4,2,16,256]{4,3,2,1,0:T(8,128)(2,1)}, s32[1,128]{1,0:T(1,128)S(1)}) custom-call(s32[1]{0:T(128)} %bitcast.refs_0_, s32[4]{0:T(128)S(1)} %get-tuple-element.21.refs_1_, f32[4]{0:T(128)S(1)} %bitcast_multiply_fusion.1.refs_2_, f32[4]{0:T(128)S(1)} %get-tuple-element.19.refs_3_, f32[128,1024]{1,0:T(8,128)S(1)} %get-tuple-element.12.refs_4_, ...), custom_call_target="tpu_custom_call" | custom-call | flops 2147483648 | bytes 4194304 | tf_op jit(solution)/shard_map/row_other/pallas_call | solution.py:225
  13.0 0.0 copy-done
  13.1 0.1 convert_reduce_fusion.1
  13.2 7.4 %all-to-all-start = ((bf16[16,4,2,16,256]{4,3,2,1,0:T(8,128)(2,1)}), bf16[16,4,2,16,256]{4,3,2,1,0:T(8,128)(2,1)S(1)}, u32[]{:S(2)}, u32[]{:S(2)}) async-start(bf16[16,4,2,16,256]{4,3,2,1,0:T(8,128)(2,1)} %get-tuple-element.15), calls=%async_computation | async-start | bytes 2097152 | tf_op jit(solution)/shard_map/all_to_all | solution.py:380
  20.6 5.2 %fusion.11.table_ref = bf16[512,1024]{1,0:T(8,128)(2,1)S(1)} fusion(s32[1024]{0:T(1024)S(1)} %get-tuple-element.23, s32[512]{0:T(512)S(1)} %get-tuple-element.28, s32[512]{0:T(512)S(1)} %get-tuple-element.30, s32[512]{0:T(512)S(1)} %get-tuple-element.29, s32[512]{0:T(512)S(1)} %get-tuple-element.33, s32[1024]{0:T(1024)S(1)} %get-tuple-element.24, ...), kind=kLoop, calls=%fused_computation.23 | loop fusion | flops 29360128 | bytes 1075712 | tf_op jit(solution)/shard_map/convert_element_type | solution.py:266
  25.9 1.5 %fusion.30.grid_ref = bf16[512,512]{1,0:T(8,128)(2,1)S(1)} fusion(s32[512]{0:T(512)S(1)} %get-tuple-element.25, s32[512]{0:T(512)S(1)} %get-tuple-element.26, pred[512]{0:T(512)(128)(4,1)S(1)} %fusion.46), kind=kLoop, calls=%fused_computation.56 | loop fusion | flops 11010048 | bytes 528896 | tf_op jit(solution)/shard_map/convert_element_type | solution.py:254
  27.4 10.2 %all-to-all-done = bf16[16,4,2,16,256]{4,3,2,1,0:T(8,128)(2,1)S(1)} async-done(((bf16[16,4,2,16,256]{4,3,2,1,0:T(8,128)(2,1)}), bf16[16,4,2,16,256]{4,3,2,1,0:T(8,128)(2,1)S(1)}, u32[]{:S(2)}, u32[]{:S(2)}) %all-to-all-start) | async-done | bytes 1048608 | tf_op jit(solution)/shard_map/all_to_all | solution.py:380
  37.6 0.9 %spread.1 = bf16[384,512]{1,0:T(8,128)(2,1)S(1)} custom-call(bf16[16,128,256]{2,1,0:T(8,128)(2,1)S(1)} %bitcast.53, bf16[512,512]{1,0:T(8,128)(2,1)S(1)} %fusion.30.grid_ref, bf16[384,128]{1,0:T(8,128)(2,1)S(1)} %fusion.36.pick_ref), custom_call_target="tpu_custom_call" | custom-call | tf_op jit(solution)/shard_map/spread/pallas_call | solution.py:307
  38.6 0.1 reshape.44
  38.7 28.1 %all_to_all.10 = bf16[128,3,4,128]{3,2,1,0:T(4,128)(2,1)S(1)} all-to-all(bf16[128,3,4,128]{3,2,1,0:T(4,128)(2,1)S(1)} %reshape.44), channel_id=1, replica_groups=mesh['facet'=128,'half'=2] {'facet'}, dimensions={0} | all-to-all | bytes 786432 | tf_op jit(solution)/shard_map/all_to_all | solution.py:393
  66.8 0.2 convert_reduce_fusion
  67.1 1.0 %finish.1 = f32[3,2,16,512]{3,2,1,0:T(8,128)} custom-call(f32[16,12,128]{2,1,0:T(8,128)S(1)} %copy.10.sum_ref, bf16[512,1024]{1,0:T(8,128)(2,1)S(1)} %fusion.11.table_ref), custom_call_target="tpu_custom_call" | custom-call | tf_op jit(solution)/shard_map/finish/pallas_call | solution.py:341
  (15 shorter events, 0.2 us)
Async XLA Ops:
  0.7 4.6 %copy-start.1 = (s32[1,8]{1,0:T(1,128)S(1)}, s32[1,8]{1,0:T(1,128)}, u32[]{:S(2)}) copy-start(s32[1,8]{1,0:T(1,128)} %param.6) | copy-start | bytes 100
  0.7 4.6 %copy-start.2 = (s32[8]{0:T(128)S(1)}, s32[8]{0:T(128)}, u32[]{:S(2)}) copy-start(s32[8]{0:T(128)} %param.7) | copy-start | bytes 100
  5.1 3.7 %collective-permute-start = (bf16[1024,512]{1,0:T(8,128)(2,1)S(1)}, bf16[1024,512]{1,0:T(8,128)(2,1)S(1)}, u32[]{:S(2)}, u32[]{:S(2)}) collective-permute-start(bf16[1024,512]{1,0:T(8,128)(2,1)S(1)} %fold.1.refs_2_), channel_id=1, source_target_pairs={{0,1},{1,0},{2,3},{3,2},{4,5},{5,4},{6,7},{7,6},{8,9},{9,8},{10,11... | collective-permute-start | bytes 3145736 | tf_op jit(solution)/shard_map/ppermute | solution.py:375
  8.8 4.2 %copy-start = (s32[2,128]{1,0:T(2,128)S(1)}, s32[2,128]{1,0:T(2,128)}, u32[]{:S(2)}) copy-start(s32[2,128]{1,0:T(2,128)} %param.9) | copy-start | bytes 3076
  13.2 24.4 %all-to-all-start = ((bf16[16,4,2,16,256]{4,3,2,1,0:T(8,128)(2,1)}), bf16[16,4,2,16,256]{4,3,2,1,0:T(8,128)(2,1)S(1)}, u32[]{:S(2)}, u32[]{:S(2)}) async-start(bf16[16,4,2,16,256]{4,3,2,1,0:T(8,128)(2,1)} %get-tuple-element.15), calls=%async_computation | async-start | bytes 2097152 | tf_op jit(solution)/shard_map/all_to_all | solution.py:380

commit v4 on v3

--- a/solution.py
+++ b/solution.py
@@ -15,11 +15,15 @@
 SUBGRIDS = 8
 CAP = 3
 NX, NZ, NY = 4, 8, 4
-GROUP = NX * NY
+PAIR = 2
+GROUP = PAIR * NX * NY
 KB = M // GROUP
+CHUNK = 2 * KB
+SLOTS = 128 // CHUNK
 FINE = 32
 SPAN = 512
 WIDTH = 16
+ROWS = WIDTH // SLOTS
 
 TWO_PI = 2.0 * math.pi
 STRIDE = IMAGE // FS
@@ -190,8 +194,8 @@
         else:
             part = part[0] + acc[n, 0], part[1] + acc[n, 1]
             y = cmul((w_re[n], w_im[n]), part)
-            for c in range(2):
-                box[n, :, c] = y[c].astype(jnp.bfloat16).reshape(GROUP, KB, M)
+            y = jnp.concatenate([t.reshape(GROUP, KB, M) for t in y], axis=1)
+            box[n] = y.astype(jnp.bfloat16)
             copies.append(pltpu.make_async_copy(box.at[n], out_ref.at[:, n], sem.at[n]))
             copies[n].start()
     if not first:
@@ -225,13 +229,13 @@
     return pl.pallas_call(
         functools.partial(row_kernel, False),
         out_shape=(
-            jax.ShapeDtypeStruct((GROUP, count, 2, KB, M), jnp.bfloat16),
+            jax.ShapeDtypeStruct((GROUP, count, CHUNK, M), jnp.bfloat16),
             jax.ShapeDtypeStruct((1, 128), jnp.int32),
         ),
         in_specs=[smem] * 4 + [vmem] * 4,
         out_specs=(pl.BlockSpec(memory_space=pltpu.HBM), vmem),
         scratch_shapes=[
-            pltpu.VMEM((count, GROUP, 2, KB, M), jnp.bfloat16),
+            pltpu.VMEM((count, GROUP, CHUNK, M), jnp.bfloat16),
             pltpu.SemaphoreType.DMA((count,)),
         ]
         + tables,
@@ -258,7 +262,8 @@
     shape = (2 * M, 2 * SG)
     row = lax.broadcasted_iota(jnp.int32, shape, 0)
     spot = lax.broadcasted_iota(jnp.int32, shape, 1) + jnp.tile(zero, (1, shape[1] // 128))
-    tick_in = order(row // (2 * KB) * KB + row % KB)
+    x, pair, y = row // (CHUNK * PAIR * NY), row // (CHUNK * NY) % PAIR, row // CHUNK % NY
+    tick_in = order(((pair * NX + x) * NY + y) * KB + row % KB)
     re, im = grid(tick_in, (spot & (SG - 1)) - SG // 2)
     part = (row // KB) & 1
     same = part == spot // SG
@@ -268,12 +273,11 @@
 
 def shuffle(rows, start):
     lane = lax.broadcasted_iota(jnp.int32, rows[0].shape, 1)
-    chunk = 128 // len(rows)
     out = None
     for n, row in enumerate(rows):
-        shift = (n - start) * chunk % 128
+        shift = (n - start) * CHUNK % 128
         row = pltpu.roll(row, shift, 1) if shift else row
-        out = row if out is None else jnp.where(lane < n * chunk, out, row)
+        out = row if out is None else jnp.where(lane < n * CHUNK, out, row)
     return out
 
 
@@ -282,9 +286,11 @@
     for n in range(1, GROUP):
         total = total + y_ref[n].astype(jnp.float32)
     turned = []
-    for n in range(0, total.shape[0], 2 * KB):
-        turned += [-total[n + KB : n + 2 * KB], total[n : n + KB]]
+    for n in range(0, total.shape[0], CHUNK):
+        turned += [-total[n + KB : n + CHUNK], total[n : n + KB]]
     both = jnp.concatenate([total, jnp.concatenate(turned, axis=0)], axis=1)
+    count = total.shape[0] // CHUNK
+    both = jnp.concatenate([both] * (SLOTS // count), axis=0)
     full[...] = lax.dot_general(
         grid_ref[...],
         both.astype(jnp.bfloat16),
@@ -292,9 +298,11 @@
         preferred_element_type=jnp.float32,
     )
     blocks = SG // WIDTH
-    for t in range(WIDTH // 4):
-        rows = [full[pl.ds(4 * q + t, blocks, stride=WIDTH), :] for q in range(4)]
-        for n in range(4):
+    for t in range(ROWS):
+        rows = [
+            full[pl.ds(ROWS * q + t, blocks, stride=WIDTH), :] for q in range(SLOTS)
+        ]
+        for n in range(count):
             part = shuffle(rows, n).astype(jnp.bfloat16)
             pieces[n * blocks : (n + 1) * blocks, t * 128 : (t + 1) * 128] = part
     out_ref[...] = jnp.dot(
@@ -306,33 +314,34 @@
     vmem = pl.BlockSpec(memory_space=pltpu.VMEM)
     return pl.pallas_call(
         spread_kernel,
-        out_shape=jax.ShapeDtypeStruct((pick.shape[0], 512), jnp.bfloat16),
+        out_shape=jax.ShapeDtypeStruct((pick.shape[0], ROWS * 128), jnp.bfloat16),
         in_specs=[vmem] * 3,
         out_specs=vmem,
         scratch_shapes=[
             pltpu.VMEM((SG, 128), jnp.float32),
-            pltpu.VMEM((128, 512), jnp.bfloat16),
+            pltpu.VMEM((pick.shape[1], ROWS * 128), jnp.bfloat16),
         ],
         compiler_params=pltpu.CompilerParams(vmem_limit_bytes=16 << 20),
         name="spread",
-    )(y.reshape(GROUP, 128, M), table, pick)
+    )(y.reshape(GROUP, -1, M), table, pick)
 
 
 def finish_kernel(scale, sum_ref, table_ref, out_ref, rows):
     rows[...] = jnp.zeros_like(rows)
     count = sum_ref.shape[1]
-    for q in range(4):
-        for g in range(GROUP // 4):
-            part = shuffle([sum_ref[4 * g + r] * scale for r in range(4)], q)
+    for q in range(SLOTS):
+        for g in range(GROUP // SLOTS):
+            part = [sum_ref[SLOTS * g + r] * scale for r in range(SLOTS)]
             at = slice(g * 128, (g + 1) * 128)
-            rows[q * 16 : q * 16 + count, at] = part.astype(jnp.bfloat16)
+            part = shuffle(part, q).astype(jnp.bfloat16)
+            rows[q * 16 : q * 16 + count, at] = part
     out = jnp.dot(rows[...], table_ref[...], preferred_element_type=jnp.float32)
-    for q in range(4):
+    for q in range(SLOTS):
         for c in range(CAP):
-            at = q * 16 + c * 4
+            at = q * 16 + c * ROWS
             for d in range(2):
-                out_ref[c, d, 4 * q : 4 * q + 4, :] = out[
-                    at : at + 4, d * SG : (d + 1) * SG
+                out_ref[c, d, ROWS * q : ROWS * (q + 1), :] = out[
+                    at : at + ROWS, d * SG : (d + 1) * SG
                 ]
 
 
@@ -343,7 +352,7 @@
         out_shape=jax.ShapeDtypeStruct((CAP, 2, WIDTH, SG), jnp.float32),
         in_specs=[vmem] * 2,
         out_specs=vmem,
-        scratch_shapes=[pltpu.VMEM((64, 2 * M), jnp.bfloat16)],
+        scratch_shapes=[pltpu.VMEM((16 * SLOTS, 2 * M), jnp.bfloat16)],
         compiler_params=pltpu.CompilerParams(vmem_limit_bytes=16 << 20),
         name="finish",
     )(total, table)
@@ -375,7 +384,13 @@
         lambda: lax.ppermute(folded, "half", [(0, 1), (1, 0)]),
     )
     groups = [
-        [(x * NZ + z) * NY + v for x in range(NX) for v in range(NY)] for z in range(NZ)
+        [
+            (x * NZ + b + z) * NY + v
+            for z in range(PAIR)
+            for x in range(NX)
+            for v in range(NY)
+        ]
+        for b in range(0, NZ, PAIR)
     ]
     y = lax.all_to_all(
         y, "facet", split_axis=0, concat_axis=0, axis_index_groups=groups, tiled=True
@@ -389,12 +404,14 @@
     target = jnp.arange(count * CAP, dtype=jnp.int32)
     pick = (target[:, None] == (owners * CAP + slot_of)[None, :]).astype(jnp.bfloat16)
     pick, last = lax.optimization_barrier((pick, finish_table(zero)))
-    outbox = spread(y, spread_table(zero), pick).reshape(count, CAP, 4, 128)
+    outbox = spread(y, spread_table(zero), pick).reshape(count, CAP, ROWS, 128)
     inbox = lax.all_to_all(outbox, "facet", split_axis=0, concat_axis=0, tiled=True)
 
     total = jnp.sum(
-        inbox.reshape(NX, NZ, NY, CAP, 4, 128), axis=1, dtype=jnp.float32
-    ).reshape(GROUP, CAP * 4, 128)
+        inbox.reshape(NX, NZ // PAIR, PAIR, NY, CAP, ROWS, 128),
+        axis=1,
+        dtype=jnp.float32,
+    ).reshape(GROUP, CAP * ROWS, 128)
     return finish(total, last, 1.0 / math.sqrt(count))[None, None]
 
 

time: 68.4 us -> 65.1 us (0.952)
  blocking collectives: 28.1 us -> 23.8 us
  waiting for transfers between devices: 10.2 us -> 8.6 us
  starting transfers between devices: 7.5 us -> 9 us
  other arithmetic: 7.32 us -> 8.43 us
    all_to_all x1, blocking collectives: 28.1 us -> 23.8 us  [shards(): lax.all_to_all(outbox, 'facet', split_axis=0, concat_axis=0, tiled=True)]
    all_to_all x1, waiting for transfers between devices: 10.2 us -> 8.59 us  [shards(): lax.all_to_all(y, 'facet', split_axis=0, concat_axis=0, axis_index_groups...]
    all_to_all x1, starting transfers between devices: 7.41 us -> 8.91 us  [shards(): lax.all_to_all(y, 'facet', split_axis=0, concat_axis=0, axis_index_groups...]
    convert_element_type x1, other arithmetic: 5.19 us -> 6.27 us  [finish_table(): return table.astype(jnp.bfloat16)]
  transfers between devices with their start and end apart: 2 -> 2, of which waited for: 1 -> 1; matrix products, arithmetic and copies ran while one was open for 10% -> 12% of each run, Pallas kernels for 5% -> 5%
where the time goes in v4:
time: 65.1 us; the launch traced here: 64.9 us
  blocking collectives  23.8 us (37%)
  Pallas kernels  14 us (22%)
  starting transfers between devices  9 us (14%)
  waiting for transfers between devices  8.6 us (13%)
  other arithmetic  8.43 us (13%)
  between operations  0.94 us (1%)
    all_to_all x1, blocking collectives, shards(): lax.all_to_all(outbox, 'facet', split_axis=0, concat_axis=0, tiled=True)  23.8 us
    all_to_all x1, starting transfers between devices, shards(): lax.all_to_all(y, 'facet', split_axis=0, concat_axis=0, axis_index_groups...  8.91 us
    all_to_all x1, waiting for transfers between devices, shards(): lax.all_to_all(y, 'facet', split_axis=0, concat_axis=0, axis_index_groups...  8.59 us
    convert_element_type x1, other arithmetic, finish_table(): return table.astype(jnp.bfloat16)  6.27 us
    pallas_call x1, Pallas kernels, fold(): pl.pallas_call(fold_kernel, out_shape=jax.ShapeDtypeStruct((rows, 2 * M),...  4.44 us
    pallas_call x1, Pallas kernels, row_product(): pl.pallas_call(functools.partial(row_kernel, False), out_shape=(jax.Shape...  4.26 us
    pallas_call x1, Pallas kernels, row_product(): pl.pallas_call(functools.partial(row_kernel, True), out_shape=(jax.ShapeD...  3.28 us
    convert_element_type x1, other arithmetic, spread_table(): return jnp.where(spot < M, re, im).astype(jnp.bfloat16)  1.54 us
  transfers between devices with their start and end apart: 2, of which 1 were waited for; matrix products, arithmetic and copies ran while one was open for 12% of the time, Pallas kernels for 5%

profile of v4, /device:TPU:8, one launch (start us, length us, event | category | flops | bytes accessed | tf_op | source)
XLA Modules:
  0.0 64.9 jit_solution(5534748039161862315)
XLA Ops:
  0.7 0.0 copy-start.1
  0.7 0.0 copy-start.2
  0.7 4.4 %fold.1.refs_2_ = bf16[1024,512]{1,0:T(8,128)(2,1)S(1)} custom-call(s32[1]{0:T(128)S(6)} %copy.11.offset_ref, bf16[1024,2048]{1,0:T(8,128)(2,1)} %bitcast.60), custom_call_target="tpu_custom_call" | custom-call | flops 2147483648 | bytes 4194304 | tf_op jit(solution)/shard_map/fold/pallas_call | solution.py:106
  5.1 0.1 collective-permute-start
  5.3 0.0 copy-done.1
  5.3 0.0 copy-done.2
  5.3 0.1 bitcast_multiply_fusion
  5.5 3.3 %row_mine.1 = (f32[4,2,256,256]{3,2,1,0:T(8,128)S(1)}, f32[128,1024]{1,0:T(8,128)S(1)}, f32[128,1024]{1,0:T(8,128)S(1)}) custom-call(s32[1]{0:T(128)} %bitcast.refs_0_, s32[4]{0:T(128)S(1)} %get-tuple-element.21.refs_1_, bf16[1024,512]{1,0:T(8,128)(2,1)S(1)} %fold.1.refs_2_), custom_call_target="tpu_custom_call" | custom-call | flops 2147483648 | bytes 4194304 | tf_op jit(solution)/shard_map/row_mine/pallas_call | solution.py:218
  8.8 0.1 bitcast_multiply_fusion.1.refs_2_
  8.9 0.0 collective-permute-done.refs_7_
  8.9 0.0 copy-start
  8.9 4.3 %row_other.1 = (bf16[32,4,16,256]{3,2,1,0:T(8,128)(2,1)}, s32[1,128]{1,0:T(1,128)S(1)}) custom-call(s32[1]{0:T(128)} %bitcast.refs_0_, s32[4]{0:T(128)S(1)} %get-tuple-element.21.refs_1_, f32[4]{0:T(128)S(1)} %bitcast_multiply_fusion.1.refs_2_, f32[4]{0:T(128)S(1)} %get-tuple-element.19.refs_3_, f32[128,1024]{1,0:T(8,128)S(1)} %get-tuple-element.12.refs_4_, ...), custom_call_target="tpu_custom_call" | custom-call | flops 2147483648 | bytes 4194304 | tf_op jit(solution)/shard_map/row_other/pallas_call | solution.py:229
  13.2 0.0 copy-done
  13.2 0.1 convert_reduce_fusion.1
  13.4 8.9 %all-to-all-start = ((bf16[32,4,16,256]{3,2,1,0:T(8,128)(2,1)}), bf16[32,4,16,256]{3,2,1,0:T(8,128)(2,1)S(1)}, u32[]{:S(2)}, u32[]{:S(2)}) async-start(bf16[32,4,16,256]{3,2,1,0:T(8,128)(2,1)} %get-tuple-element.15), calls=%async_computation | async-start | bytes 2097152 | tf_op jit(solution)/shard_map/all_to_all | solution.py:395
  22.3 6.3 %fusion.17.table_ref = bf16[512,1024]{1,0:T(8,128)(2,1)S(1)} fusion(s32[1024]{0:T(1024)S(1)} %get-tuple-element.23, s32[512]{0:T(512)S(1)} %get-tuple-element.31, s32[512]{0:T(512)S(1)} %get-tuple-element.32, s32[512]{0:T(512)S(1)} %get-tuple-element.27, s32[512]{0:T(512)S(1)} %get-tuple-element.37, s32[512]{0:T(512)S(1)} %get-tuple-element.28, ...), kind=kLoop, calls=%fused_computation.39 | loop fusion | flops 44040192 | bytes 1084928 | tf_op jit(solution)/shard_map/convert_element_type | solution.py:271
  28.6 1.5 %fusion.38.grid_ref = bf16[512,512]{1,0:T(8,128)(2,1)S(1)} fusion(s32[512]{0:T(512)S(1)} %get-tuple-element.25, s32[512]{0:T(512)S(1)} %get-tuple-element.26, pred[512]{0:T(512)(128)(4,1)S(1)} %fusion.56), kind=kLoop, calls=%fused_computation.74 | loop fusion | flops 11010048 | bytes 528896 | tf_op jit(solution)/shard_map/convert_element_type | solution.py:258
  30.1 8.6 %all-to-all-done = bf16[32,4,16,256]{3,2,1,0:T(8,128)(2,1)S(1)} async-done(((bf16[32,4,16,256]{3,2,1,0:T(8,128)(2,1)}), bf16[32,4,16,256]{3,2,1,0:T(8,128)(2,1)S(1)}, u32[]{:S(2)}, u32[]{:S(2)}) %all-to-all-start) | async-done | bytes 1048608 | tf_op jit(solution)/shard_map/all_to_all | solution.py:395
  38.7 0.9 %spread.1 = bf16[384,256]{1,0:T(8,128)(2,1)S(1)} custom-call(bf16[32,64,256]{2,1,0:T(8,128)(2,1)S(1)} %bitcast.53, bf16[512,512]{1,0:T(8,128)(2,1)S(1)} %fusion.38.grid_ref, bf16[384,128]{1,0:T(8,128)(2,1)S(1)} %fusion.44.pick_ref), custom_call_target="tpu_custom_call" | custom-call | tf_op jit(solution)/shard_map/spread/pallas_call | solution.py:315
  39.6 0.1 reshape.44
  39.7 23.8 %all_to_all.10 = bf16[128,3,2,128]{3,2,1,0:T(2,128)(2,1)S(1)} all-to-all(bf16[128,3,2,128]{3,2,1,0:T(2,128)(2,1)S(1)} %reshape.44), channel_id=1, replica_groups=mesh['facet'=128,'half'=2] {'facet'}, dimensions={0} | all-to-all | bytes 393216 | tf_op jit(solution)/shard_map/all_to_all | solution.py:408
  63.5 0.2 convert_reduce_fusion
  63.7 0.1 copy.10.sum_ref
  63.8 1.1 %finish.1 = f32[3,2,16,512]{3,2,1,0:T(8,128)} custom-call(f32[32,6,128]{2,1,0:T(8,128)S(1)} %copy.10.sum_ref, bf16[512,1024]{1,0:T(8,128)(2,1)S(1)} %fusion.17.table_ref), custom_call_target="tpu_custom_call" | custom-call | tf_op jit(solution)/shard_map/finish/pallas_call | solution.py:350
  (17 shorter events, 0.2 us)
Async XLA Ops:
  0.7 4.7 %copy-start.1 = (s32[1,8]{1,0:T(1,128)S(1)}, s32[1,8]{1,0:T(1,128)}, u32[]{:S(2)}) copy-start(s32[1,8]{1,0:T(1,128)} %param.6) | copy-start | bytes 100
  0.7 4.7 %copy-start.2 = (s32[8]{0:T(128)S(1)}, s32[8]{0:T(128)}, u32[]{:S(2)}) copy-start(s32[8]{0:T(128)} %param.7) | copy-start | bytes 100
  5.1 3.7 %collective-permute-start = (bf16[1024,512]{1,0:T(8,128)(2,1)S(1)}, bf16[1024,512]{1,0:T(8,128)(2,1)S(1)}, u32[]{:S(2)}, u32[]{:S(2)}) collective-permute-start(bf16[1024,512]{1,0:T(8,128)(2,1)S(1)} %fold.1.refs_2_), channel_id=1, source_target_pairs={{0,1},{1,0},{2,3},{3,2},{4,5},{5,4},{6,7},{7,6},{8,9},{9,8},{10,11... | collective-permute-start | bytes 3145736 | tf_op jit(solution)/shard_map/ppermute | solution.py:384
  8.9 4.3 %copy-start = (s32[2,128]{1,0:T(2,128)S(1)}, s32[2,128]{1,0:T(2,128)}, u32[]{:S(2)}) copy-start(s32[2,128]{1,0:T(2,128)} %param.9) | copy-start | bytes 3076
  13.4 25.4 %all-to-all-start = ((bf16[32,4,16,256]{3,2,1,0:T(8,128)(2,1)}), bf16[32,4,16,256]{3,2,1,0:T(8,128)(2,1)S(1)}, u32[]{:S(2)}, u32[]{:S(2)}) async-start(bf16[32,4,16,256]{3,2,1,0:T(8,128)(2,1)} %get-tuple-element.15), calls=%async_computation | async-start | bytes 2097152 | tf_op jit(solution)/shard_map/all_to_all | solution.py:395

commit v5 on v4

--- a/solution.py
+++ b/solution.py
@@ -21,7 +21,7 @@
 CHUNK = 2 * KB
 SLOTS = 128 // CHUNK
 FINE = 32
-SPAN = 512
+SPAN = 256
 WIDTH = 16
 ROWS = WIDTH // SLOTS
 
@@ -56,11 +56,10 @@
 
 
 def fold_kernel(offset_ref, x_hbm, out_ref, big_re, big_im, *scratch):
-    steps = FS // SPAN
-    images, tables, sem = scratch[:steps], scratch[steps : 2 * steps], scratch[-1]
+    *images, table, sem = scratch
     copies = [
-        pltpu.make_async_copy(x_hbm.at[:, pl.ds(n * SPAN, SPAN)], images[n], sem.at[n])
-        for n in range(steps)
+        pltpu.make_async_copy(x_hbm.at[pl.ds(n * SPAN, SPAN)], image, sem.at[n])
+        for n, image in enumerate(images)
     ]
     for copy in copies:
         copy.start()
@@ -76,33 +75,24 @@
     small = wave(FINE, 1, 0)
     row = lax.broadcasted_iota(jnp.int32, (FINE, 128), 0)
 
-    def make(n):
-        for m in range(SPAN // FINE):
-            at = n * (SPAN // FINE) + m
-            big = big_re[at : at + 1, :], big_im[at : at + 1, :]
-            taper = taper_of(row + (at * FINE - FS // 2))
-            taper = jnp.concatenate([taper, taper], axis=1)
-            re, im = cmul(big, small)
-            rows = slice(m * FINE, (m + 1) * FINE)
-            tables[n][rows, :M] = (taper * re).astype(jnp.bfloat16)
-            tables[n][rows, M:] = (taper * im).astype(jnp.bfloat16)
-
-    make(0)
-    total = None
-    for n in range(steps):
+    for n in range(FS // FINE):
+        big = big_re[n : n + 1, :], big_im[n : n + 1, :]
+        taper = taper_of(row + (n * FINE - FS // 2))
+        taper = jnp.concatenate([taper, taper], axis=1)
+        re, im = cmul(big, small)
+        rows = slice(n * FINE, (n + 1) * FINE)
+        table[rows, :M] = (taper * re).astype(jnp.bfloat16)
+        table[rows, M:] = (taper * im).astype(jnp.bfloat16)
+    for n, image in enumerate(images):
         copies[n].wait()
-        if n + 1 < steps:
-            make(n + 1)
-        term = jnp.dot(
-            images[n][...], tables[n][...], preferred_element_type=jnp.float32
-        )
-        total = term if total is None else total + term
-    out_ref[...] = total.astype(jnp.bfloat16)
+        out_ref[n * SPAN : (n + 1) * SPAN] = jnp.dot(
+            image[...], table[...], preferred_element_type=jnp.float32
+        ).astype(jnp.bfloat16)
 
 
 def fold(pixels, column_offset):
     rows = pixels.shape[0]
-    steps = FS // SPAN
+    steps = rows // SPAN
     return pl.pallas_call(
         fold_kernel,
         out_shape=jax.ShapeDtypeStruct((rows, 2 * M), jnp.bfloat16),
@@ -115,8 +105,8 @@
             pltpu.VMEM((FS // FINE, M), jnp.float32),
             pltpu.VMEM((FS // FINE, M), jnp.float32),
         ]
-        + [pltpu.VMEM((rows, SPAN), jnp.bfloat16)] * steps
-        + [pltpu.VMEM((SPAN, 2 * M), jnp.bfloat16)] * steps
+        + [pltpu.VMEM((SPAN, FS), jnp.bfloat16)] * steps
+        + [pltpu.VMEM((FS, 2 * M), jnp.bfloat16)]
         + [pltpu.SemaphoreType.DMA((steps,))],
         cost_estimate=pl.CostEstimate(
             flops=4 * rows * FS * M, bytes_accessed=rows * FS * 2, transcendentals=0

time: 65.1 us -> 64.8 us (level)
  no operation moved by 1% of the time
where the time goes in v5:
time: 64.8 us; the launch traced here: 64.5 us
  blocking collectives  23.8 us (37%)
  Pallas kernels  13.6 us (21%)
  starting transfers between devices  8.99 us (14%)
  waiting for transfers between devices  8.59 us (13%)
  other arithmetic  8.43 us (13%)
  between operations  0.94 us (1%)
    all_to_all x1, blocking collectives, shards(): lax.all_to_all(outbox, 'facet', split_axis=0, concat_axis=0, tiled=True)  23.8 us
    all_to_all x1, starting transfers between devices, shards(): lax.all_to_all(y, 'facet', split_axis=0, concat_axis=0, axis_index_groups...  8.9 us
    all_to_all x1, waiting for transfers between devices, shards(): lax.all_to_all(y, 'facet', split_axis=0, concat_axis=0, axis_index_groups...  8.59 us
    convert_element_type x1, other arithmetic, finish_table(): return table.astype(jnp.bfloat16)  6.27 us
    pallas_call x1, Pallas kernels, row_product(): pl.pallas_call(functools.partial(row_kernel, False), out_shape=(jax.Shape...  4.27 us
    pallas_call x1, Pallas kernels, fold(): pl.pallas_call(fold_kernel, out_shape=jax.ShapeDtypeStruct((rows, 2 * M),...  4.1 us
    pallas_call x1, Pallas kernels, row_product(): pl.pallas_call(functools.partial(row_kernel, True), out_shape=(jax.ShapeD...  3.28 us
    convert_element_type x1, other arithmetic, spread_table(): return jnp.where(spot < M, re, im).astype(jnp.bfloat16)  1.54 us
  transfers between devices with their start and end apart: 2, of which 1 were waited for; matrix products, arithmetic and copies ran while one was open for 12% of the time, Pallas kernels for 5%

profile of v5, /device:TPU:8, one launch (start us, length us, event | category | flops | bytes accessed | tf_op | source)
XLA Modules:
  0.0 64.5 jit_solution(12853749350840411134)
XLA Ops:
  0.7 0.0 copy-start.1
  0.7 0.0 copy-start.2
  0.7 4.1 %fold.1.refs_2_ = bf16[1024,512]{1,0:T(8,128)(2,1)S(1)} custom-call(s32[1]{0:T(128)S(6)} %copy.11.offset_ref, bf16[1024,2048]{1,0:T(8,128)(2,1)} %bitcast.60), custom_call_target="tpu_custom_call" | custom-call | flops 2147483648 | bytes 4194304 | tf_op jit(solution)/shard_map/fold/pallas_call | solution.py:96
  4.8 0.1 collective-permute-start
  5.0 0.0 copy-done.1
  5.0 0.0 copy-done.2
  5.0 0.1 bitcast_multiply_fusion
  5.2 3.3 %row_mine.1 = (f32[4,2,256,256]{3,2,1,0:T(8,128)S(1)}, f32[128,1024]{1,0:T(8,128)S(1)}, f32[128,1024]{1,0:T(8,128)S(1)}) custom-call(s32[1]{0:T(128)} %bitcast.refs_0_, s32[4]{0:T(128)S(1)} %get-tuple-element.21.refs_1_, bf16[1024,512]{1,0:T(8,128)(2,1)S(1)} %fold.1.refs_2_), custom_call_target="tpu_custom_call" | custom-call | flops 2147483648 | bytes 4194304 | tf_op jit(solution)/shard_map/row_mine/pallas_call | solution.py:208
  8.4 0.1 bitcast_multiply_fusion.1.refs_2_
  8.5 0.0 collective-permute-done.refs_7_
  8.5 0.0 copy-start
  8.5 4.3 %row_other.1 = (bf16[32,4,16,256]{3,2,1,0:T(8,128)(2,1)}, s32[1,128]{1,0:T(1,128)S(1)}) custom-call(s32[1]{0:T(128)} %bitcast.refs_0_, s32[4]{0:T(128)S(1)} %get-tuple-element.21.refs_1_, f32[4]{0:T(128)S(1)} %bitcast_multiply_fusion.1.refs_2_, f32[4]{0:T(128)S(1)} %get-tuple-element.19.refs_3_, f32[128,1024]{1,0:T(8,128)S(1)} %get-tuple-element.12.refs_4_, ...), custom_call_target="tpu_custom_call" | custom-call | flops 2147483648 | bytes 4194304 | tf_op jit(solution)/shard_map/row_other/pallas_call | solution.py:219
  12.8 0.0 copy-done
  12.9 0.1 convert_reduce_fusion.1
  13.0 8.9 %all-to-all-start = ((bf16[32,4,16,256]{3,2,1,0:T(8,128)(2,1)}), bf16[32,4,16,256]{3,2,1,0:T(8,128)(2,1)S(1)}, u32[]{:S(2)}, u32[]{:S(2)}) async-start(bf16[32,4,16,256]{3,2,1,0:T(8,128)(2,1)} %get-tuple-element.15), calls=%async_computation | async-start | bytes 2097152 | tf_op jit(solution)/shard_map/all_to_all | solution.py:385
  22.0 6.3 %fusion.17.table_ref = bf16[512,1024]{1,0:T(8,128)(2,1)S(1)} fusion(s32[1024]{0:T(1024)S(1)} %get-tuple-element.23, s32[512]{0:T(512)S(1)} %get-tuple-element.31, s32[512]{0:T(512)S(1)} %get-tuple-element.32, s32[512]{0:T(512)S(1)} %get-tuple-element.27, s32[512]{0:T(512)S(1)} %get-tuple-element.37, s32[512]{0:T(512)S(1)} %get-tuple-element.28, ...), kind=kLoop, calls=%fused_computation.39 | loop fusion | flops 44040192 | bytes 1084928 | tf_op jit(solution)/shard_map/convert_element_type | solution.py:261
  28.3 1.5 %fusion.38.grid_ref = bf16[512,512]{1,0:T(8,128)(2,1)S(1)} fusion(s32[512]{0:T(512)S(1)} %get-tuple-element.25, s32[512]{0:T(512)S(1)} %get-tuple-element.26, pred[512]{0:T(512)(128)(4,1)S(1)} %fusion.56), kind=kLoop, calls=%fused_computation.74 | loop fusion | flops 11010048 | bytes 528896 | tf_op jit(solution)/shard_map/convert_element_type | solution.py:248
  29.8 8.6 %all-to-all-done = bf16[32,4,16,256]{3,2,1,0:T(8,128)(2,1)S(1)} async-done(((bf16[32,4,16,256]{3,2,1,0:T(8,128)(2,1)}), bf16[32,4,16,256]{3,2,1,0:T(8,128)(2,1)S(1)}, u32[]{:S(2)}, u32[]{:S(2)}) %all-to-all-start) | async-done | bytes 1048608 | tf_op jit(solution)/shard_map/all_to_all | solution.py:385
  38.4 0.9 %spread.1 = bf16[384,256]{1,0:T(8,128)(2,1)S(1)} custom-call(bf16[32,64,256]{2,1,0:T(8,128)(2,1)S(1)} %bitcast.53, bf16[512,512]{1,0:T(8,128)(2,1)S(1)} %fusion.38.grid_ref, bf16[384,128]{1,0:T(8,128)(2,1)S(1)} %fusion.44.pick_ref), custom_call_target="tpu_custom_call" | custom-call | tf_op jit(solution)/shard_map/spread/pallas_call | solution.py:305
  39.3 0.1 reshape.44
  39.4 23.8 %all_to_all.10 = bf16[128,3,2,128]{3,2,1,0:T(2,128)(2,1)S(1)} all-to-all(bf16[128,3,2,128]{3,2,1,0:T(2,128)(2,1)S(1)} %reshape.44), channel_id=1, replica_groups=mesh['facet'=128,'half'=2] {'facet'}, dimensions={0} | all-to-all | bytes 393216 | tf_op jit(solution)/shard_map/all_to_all | solution.py:398
  63.1 0.2 convert_reduce_fusion
  63.4 0.1 copy.10.sum_ref
  63.4 1.1 %finish.1 = f32[3,2,16,512]{3,2,1,0:T(8,128)} custom-call(f32[32,6,128]{2,1,0:T(8,128)S(1)} %copy.10.sum_ref, bf16[512,1024]{1,0:T(8,128)(2,1)S(1)} %fusion.17.table_ref), custom_call_target="tpu_custom_call" | custom-call | tf_op jit(solution)/shard_map/finish/pallas_call | solution.py:340
  (17 shorter events, 0.2 us)
Async XLA Ops:
  0.7 4.3 %copy-start.1 = (s32[1,8]{1,0:T(1,128)S(1)}, s32[1,8]{1,0:T(1,128)}, u32[]{:S(2)}) copy-start(s32[1,8]{1,0:T(1,128)} %param.6) | copy-start | bytes 100
  0.7 4.3 %copy-start.2 = (s32[8]{0:T(128)S(1)}, s32[8]{0:T(128)}, u32[]{:S(2)}) copy-start(s32[8]{0:T(128)} %param.7) | copy-start | bytes 100
  4.8 3.7 %collective-permute-start = (bf16[1024,512]{1,0:T(8,128)(2,1)S(1)}, bf16[1024,512]{1,0:T(8,128)(2,1)S(1)}, u32[]{:S(2)}, u32[]{:S(2)}) collective-permute-start(bf16[1024,512]{1,0:T(8,128)(2,1)S(1)} %fold.1.refs_2_), channel_id=1, source_target_pairs={{0,1},{1,0},{2,3},{3,2},{4,5},{5,4},{6,7},{7,6},{8,9},{9,8},{10,11... | collective-permute-start | bytes 3145736 | tf_op jit(solution)/shard_map/ppermute | solution.py:374
  8.5 4.3 %copy-start = (s32[2,128]{1,0:T(2,128)S(1)}, s32[2,128]{1,0:T(2,128)}, u32[]{:S(2)}) copy-start(s32[2,128]{1,0:T(2,128)} %param.9) | copy-start | bytes 3076
  13.0 25.4 %all-to-all-start = ((bf16[32,4,16,256]{3,2,1,0:T(8,128)(2,1)}), bf16[32,4,16,256]{3,2,1,0:T(8,128)(2,1)S(1)}, u32[]{:S(2)}, u32[]{:S(2)}) async-start(bf16[32,4,16,256]{3,2,1,0:T(8,128)(2,1)} %get-tuple-element.15), calls=%async_computation | async-start | bytes 2097152 | tf_op jit(solution)/shard_map/all_to_all | solution.py:385

commit v6 on v5

--- a/solution.py
+++ b/solution.py
@@ -386,14 +386,16 @@
         y, "facet", split_axis=0, concat_axis=0, axis_index_groups=groups, tiled=True
     )
 
-    owners = lax.dynamic_index_in_dim(piece_owner, half, 0, keepdims=False) + zero[0]
+    last = finish_table(zero)
+    owners = lax.dynamic_index_in_dim(piece_owner, half, 0, keepdims=False)
+    owners = owners + (last[0, :128].astype(jnp.float32) * 0.0).astype(jnp.int32)
     count = owners.shape[0]
     place = jnp.arange(count, dtype=jnp.int32)
     same = (owners[:, None] == owners[None, :]) & (place[:, None] < place[None, :])
     slot_of = jnp.sum(same.astype(jnp.int32), axis=0)
     target = jnp.arange(count * CAP, dtype=jnp.int32)
     pick = (target[:, None] == (owners * CAP + slot_of)[None, :]).astype(jnp.bfloat16)
-    pick, last = lax.optimization_barrier((pick, finish_table(zero)))
+    pick, last = lax.optimization_barrier((pick, last))
     outbox = spread(y, spread_table(zero), pick).reshape(count, CAP, ROWS, 128)
     inbox = lax.all_to_all(outbox, "facet", split_axis=0, concat_axis=0, tiled=True)
 

time: 64.8 us -> 64.6 us (level)
  transfers between devices with their start and end apart: 2 -> 2, of which waited for: 1 -> 1; matrix products, arithmetic and copies ran while one was open for 12% -> 13% of each run, Pallas kernels for 5% -> 5%
where the time goes in v6:
time: 64.6 us; the launch traced here: 64.3 us
  blocking collectives  23.8 us (37%)
  Pallas kernels  13.6 us (21%)
  starting transfers between devices  8.98 us (14%)
  other arithmetic  8.42 us (13%)
  waiting for transfers between devices  8.42 us (13%)
  between operations  0.94 us (1%)
    all_to_all x1, blocking collectives, shards(): lax.all_to_all(outbox, 'facet', split_axis=0, concat_axis=0, tiled=True)  23.8 us
    all_to_all x1, starting transfers between devices, shards(): lax.all_to_all(y, 'facet', split_axis=0, concat_axis=0, axis_index_groups...  8.89 us
    all_to_all x1, waiting for transfers between devices, shards(): lax.all_to_all(y, 'facet', split_axis=0, concat_axis=0, axis_index_groups...  8.42 us
    convert_element_type x1, other arithmetic, finish_table(): return table.astype(jnp.bfloat16)  6.28 us
    pallas_call x1, Pallas kernels, row_product(): pl.pallas_call(functools.partial(row_kernel, False), out_shape=(jax.Shape...  4.27 us
    pallas_call x1, Pallas kernels, fold(): pl.pallas_call(fold_kernel, out_shape=jax.ShapeDtypeStruct((rows, 2 * M),...  4.1 us
    pallas_call x1, Pallas kernels, row_product(): pl.pallas_call(functools.partial(row_kernel, True), out_shape=(jax.ShapeD...  3.28 us
    convert_element_type x1, other arithmetic, spread_table(): return jnp.where(spot < M, re, im).astype(jnp.bfloat16)  1.54 us
  transfers between devices with their start and end apart: 2, of which 1 were waited for; matrix products, arithmetic and copies ran while one was open for 13% of the time, Pallas kernels for 5%

profile of v6, /device:TPU:8, one launch (start us, length us, event | category | flops | bytes accessed | tf_op | source)
XLA Modules:
  0.0 64.3 jit_solution(4845760926494283613)
XLA Ops:
  0.7 0.0 copy-start
  0.7 0.0 copy-start.1
  0.7 4.1 %fold.1.refs_2_ = bf16[1024,512]{1,0:T(8,128)(2,1)S(1)} custom-call(s32[1]{0:T(128)S(6)} %copy.11.offset_ref, bf16[1024,2048]{1,0:T(8,128)(2,1)} %bitcast.57), custom_call_target="tpu_custom_call" | custom-call | flops 2147483648 | bytes 4194304 | tf_op jit(solution)/shard_map/fold/pallas_call | solution.py:96
  4.8 0.1 collective-permute-start
  5.0 0.0 copy-done
  5.0 0.0 copy-done.1
  5.0 0.1 bitcast_multiply_fusion
  5.2 3.3 %row_mine.1 = (f32[4,2,256,256]{3,2,1,0:T(8,128)S(1)}, f32[128,1024]{1,0:T(8,128)S(1)}, f32[128,1024]{1,0:T(8,128)S(1)}) custom-call(s32[1]{0:T(128)} %bitcast.refs_0_, s32[4]{0:T(128)S(1)} %get-tuple-element.21.refs_1_, bf16[1024,512]{1,0:T(8,128)(2,1)S(1)} %fold.1.refs_2_), custom_call_target="tpu_custom_call" | custom-call | flops 2147483648 | bytes 4194304 | tf_op jit(solution)/shard_map/row_mine/pallas_call | solution.py:208
  8.4 0.1 bitcast_multiply_fusion.1.refs_2_
  8.5 0.0 collective-permute-done.refs_7_
  8.5 4.3 %row_other.1 = (bf16[32,4,16,256]{3,2,1,0:T(8,128)(2,1)}, s32[1,128]{1,0:T(1,128)S(1)}) custom-call(s32[1]{0:T(128)} %bitcast.refs_0_, s32[4]{0:T(128)S(1)} %get-tuple-element.21.refs_1_, f32[4]{0:T(128)S(1)} %bitcast_multiply_fusion.1.refs_2_, f32[4]{0:T(128)S(1)} %get-tuple-element.19.refs_3_, f32[128,1024]{1,0:T(8,128)S(1)} %get-tuple-element.12.refs_4_, ...), custom_call_target="tpu_custom_call" | custom-call | flops 2147483648 | bytes 4194304 | tf_op jit(solution)/shard_map/row_other/pallas_call | solution.py:219
  12.8 0.0 copy-start.2
  12.9 8.9 %all-to-all-start = ((bf16[32,4,16,256]{3,2,1,0:T(8,128)(2,1)}), bf16[32,4,16,256]{3,2,1,0:T(8,128)(2,1)S(1)}, u32[]{:S(2)}, u32[]{:S(2)}) async-start(bf16[32,4,16,256]{3,2,1,0:T(8,128)(2,1)} %get-tuple-element.15), calls=%async_computation | async-start | bytes 2097152 | tf_op jit(solution)/shard_map/all_to_all | solution.py:385
  21.8 6.3 %fusion.17.table_ref = bf16[512,1024]{1,0:T(8,128)(2,1)S(1)} fusion(s32[1024]{0:T(1024)S(1)} %get-tuple-element.23, s32[512]{0:T(512)S(1)} %get-tuple-element.31, s32[512]{0:T(512)S(1)} %get-tuple-element.32, s32[512]{0:T(512)S(1)} %get-tuple-element.27, s32[512]{0:T(512)S(1)} %get-tuple-element.37, s32[512]{0:T(512)S(1)} %get-tuple-element.28, ...), kind=kLoop, calls=%fused_computation.39 | loop fusion | flops 44040192 | bytes 1084928 | tf_op jit(solution)/shard_map/convert_element_type | solution.py:261
  28.0 0.0 copy-done.2
  28.1 0.1 convert_reduce_fusion.1
  28.2 1.5 %fusion.38.grid_ref = bf16[512,512]{1,0:T(8,128)(2,1)S(1)} fusion(s32[512]{0:T(512)S(1)} %get-tuple-element.25, s32[512]{0:T(512)S(1)} %get-tuple-element.26, pred[512]{0:T(512)(128)(4,1)S(1)} %fusion.56), kind=kLoop, calls=%fused_computation.74 | loop fusion | flops 11010048 | bytes 528896 | tf_op jit(solution)/shard_map/convert_element_type | solution.py:248
  29.8 8.4 %all-to-all-done = bf16[32,4,16,256]{3,2,1,0:T(8,128)(2,1)S(1)} async-done(((bf16[32,4,16,256]{3,2,1,0:T(8,128)(2,1)}), bf16[32,4,16,256]{3,2,1,0:T(8,128)(2,1)S(1)}, u32[]{:S(2)}, u32[]{:S(2)}) %all-to-all-start) | async-done | bytes 1048608 | tf_op jit(solution)/shard_map/all_to_all | solution.py:385
  38.2 0.9 %spread.1 = bf16[384,256]{1,0:T(8,128)(2,1)S(1)} custom-call(bf16[32,64,256]{2,1,0:T(8,128)(2,1)S(1)} %bitcast.49, bf16[512,512]{1,0:T(8,128)(2,1)S(1)} %fusion.38.grid_ref, bf16[384,128]{1,0:T(8,128)(2,1)S(1)} %fusion.44.pick_ref), custom_call_target="tpu_custom_call" | custom-call | tf_op jit(solution)/shard_map/spread/pallas_call | solution.py:305
  39.1 0.1 reshape.52
  39.1 23.8 %all_to_all.10 = bf16[128,3,2,128]{3,2,1,0:T(2,128)(2,1)S(1)} all-to-all(bf16[128,3,2,128]{3,2,1,0:T(2,128)(2,1)S(1)} %reshape.52), channel_id=1, replica_groups=mesh['facet'=128,'half'=2] {'facet'}, dimensions={0} | all-to-all | bytes 393216 | tf_op jit(solution)/shard_map/all_to_all | solution.py:400
  62.9 0.2 convert_reduce_fusion
  63.2 0.1 copy.10.sum_ref
  63.2 1.1 %finish.1 = f32[3,2,16,512]{3,2,1,0:T(8,128)} custom-call(f32[32,6,128]{2,1,0:T(8,128)S(1)} %copy.10.sum_ref, bf16[512,1024]{1,0:T(8,128)(2,1)S(1)} %fusion.17.table_ref), custom_call_target="tpu_custom_call" | custom-call | tf_op jit(solution)/shard_map/finish/pallas_call | solution.py:340
  (16 shorter events, 0.2 us)
Async XLA Ops:
  0.7 4.3 %copy-start = (s32[1,8]{1,0:T(1,128)S(1)}, s32[1,8]{1,0:T(1,128)}, u32[]{:S(2)}) copy-start(s32[1,8]{1,0:T(1,128)} %param.6) | copy-start | bytes 100
  0.7 4.3 %copy-start.1 = (s32[8]{0:T(128)S(1)}, s32[8]{0:T(128)}, u32[]{:S(2)}) copy-start(s32[8]{0:T(128)} %param.7) | copy-start | bytes 100
  4.8 3.7 %collective-permute-start = (bf16[1024,512]{1,0:T(8,128)(2,1)S(1)}, bf16[1024,512]{1,0:T(8,128)(2,1)S(1)}, u32[]{:S(2)}, u32[]{:S(2)}) collective-permute-start(bf16[1024,512]{1,0:T(8,128)(2,1)S(1)} %fold.1.refs_2_), channel_id=1, source_target_pairs={{0,1},{1,0},{2,3},{3,2},{4,5},{5,4},{6,7},{7,6},{8,9},{9,8},{10,11... | collective-permute-start | bytes 3145736 | tf_op jit(solution)/shard_map/ppermute | solution.py:374
  12.8 15.2 %copy-start.2 = (s32[2,128]{1,0:T(2,128)S(1)}, s32[2,128]{1,0:T(2,128)}, u32[]{:S(2)}) copy-start(s32[2,128]{1,0:T(2,128)} %param.9) | copy-start | bytes 3076
  12.9 25.4 %all-to-all-start = ((bf16[32,4,16,256]{3,2,1,0:T(8,128)(2,1)}), bf16[32,4,16,256]{3,2,1,0:T(8,128)(2,1)S(1)}, u32[]{:S(2)}, u32[]{:S(2)}) async-start(bf16[32,4,16,256]{3,2,1,0:T(8,128)(2,1)} %get-tuple-element.15), calls=%async_computation | async-start | bytes 2097152 | tf_op jit(solution)/shard_map/all_to_all | solution.py:385
